TPU v7x, 256 devices: a whole 4x4x8 slice. The times are simulated.
256 devices in a mesh: dp: 8 (over x, core), seq: 32 (over y, z).
Axes of the slice: x: 4, y: 4, z: 8, core: 2. Of those that a mesh axis runs over, the one named last changes fastest.
Arguments:
- q_lin: bfloat16 [32768, 256], P(('dp', 'seq')), parts along dimension 0, may hold values from -9 to 9
- k_lin: bfloat16 [32768, 256], P(('dp', 'seq')), parts along dimension 0, may hold values from -9 to 9
- q_win: bfloat16 [32768, 1024], P(('dp', 'seq')), parts along dimension 0, may hold values from -6 to 6
- k_win: bfloat16 [32768, 1024], P(('dp', 'seq')), parts along dimension 0, may hold values from -6 to 6
- values: bfloat16 [32768, 1024], P(('dp', 'seq')), parts along dimension 0, may hold values from -8 to 8
- grad_out: bfloat16 [32768, 1024], P(('dp', 'seq')), parts along dimension 0, may hold values from -8 to 8
Outputs:
- mixed: bfloat16 [32768, 1024], P(('dp', 'seq')), parts along dimension 0
- grad_q_lin: bfloat16 [32768, 256], P(('dp', 'seq')), parts along dimension 0
- grad_k_lin: bfloat16 [32768, 256], P(('dp', 'seq')), parts along dimension 0
- grad_q_win: bfloat16 [32768, 1024], P(('dp', 'seq')), parts along dimension 0
- grad_k_win: bfloat16 [32768, 1024], P(('dp', 'seq')), parts along dimension 0
- grad_values: bfloat16 [32768, 1024], P(('dp', 'seq')), parts along dimension 0
There are 8 independent parts, one for each index of `dp`. A program takes and returns all parts, laid end to end along the dimension named above; each array names one. Nothing has to cross between parts.
All inputs are finite; a program needn't handle non-finite values.
Results may differ from a plain program's by a relative error of at most 0.0091.
Values may be sent and summed in bfloat16 or wider, within the bound.
No kernel may reach another device: no remote copies, remote signals or barrier semaphores. Data moves between devices by JAX's collectives and lax.ppermute only.
A program may use at most 192 MiB of HBM per device.

v0:
```python
import math

import jax
import jax.numpy as jnp
from jax import lax
from jax.sharding import PartitionSpec as P

H = 16
DH = 64
FD = 16
WINDOW = 128


HIGH = lax.Precision.HIGH


def carried_in(part, axis, combine, identity, reverse):
    count = lax.axis_size(axis)
    place = lax.axis_index(axis)
    ahead = count - 1 - place if reverse else place
    gathered = jax.tree.map(lambda a: lax.all_gather(a, axis), part)
    state = jax.tree.map(lambda a, e: jnp.zeros_like(a) + jnp.asarray(e, a.dtype), part, identity)

    def one(turn, state):
        source = count - 1 - turn if reverse else turn
        return combine(
            state, jax.tree.map(lambda a: lax.dynamic_index_in_dim(a, source, 0, False), gathered)
        )

    return lax.fori_loop(0, ahead, one, state)


def passed_along(value, axis, steps):
    count = lax.axis_size(axis)
    leading, last = (max(0, -steps), min(count, count - steps))
    return lax.ppermute(value, axis, [(source, source + steps) for source in range(leading, last)])


def feat_full(inputs):
    feat_depth = inputs.shape[-1]
    leading = inputs.shape[:-1]
    ones_col = jnp.ones(leading + (1,), inputs.dtype)
    square = (inputs[..., :, None] * inputs[..., None, :]).reshape(
        leading + (feat_depth * feat_depth,)
    )
    linear_factor = 1.0 / math.sqrt(math.sqrt(feat_depth))
    return jnp.concatenate(
        [ones_col, inputs * linear_factor, square / math.sqrt(2.0 * feat_depth)], -1
    )


def linear_pieces(query_low, key_low):
    inv_root = 1.0 / math.sqrt(query_low.shape[-1])
    scores = (
        jnp.einsum("thf,shf->hts", query_low, key_low, preferred_element_type=jnp.float32)
        * inv_root
    )
    tok_count = query_low.shape[0]
    causal = (
        jnp.arange(tok_count, dtype=jnp.int32)[:, None]
        >= jnp.arange(tok_count, dtype=jnp.int32)[None, :]
    )
    kernel = jnp.where(causal[None], 1.0 + scores + 0.5 * scores * scores, 0.0)
    return (scores, kernel, causal)


def linear_grads(
    lin_query,
    lin_key,
    value_f32,
    d_numer,
    d_denom,
    prev_state,
    prev_norm,
    next_state,
    next_norm,
    scores,
    kernel,
    causal,
    key_feat,
    query_pull,
    key_pull,
):
    inv_root = 1.0 / math.sqrt(lin_query.shape[-1])
    d_kernel = (
        jnp.einsum("thd,shd->hts", d_numer, value_f32, precision=HIGH) + d_denom.T[:, :, None]
    )
    d_scores = jnp.where(causal[None], d_kernel, 0.0) * (1.0 + scores)
    d_values = jnp.einsum("hts,thd->shd", kernel, d_numer, precision=HIGH) + jnp.einsum(
        "shf,hfd->shd", key_feat, next_state, precision=HIGH
    )
    d_qfeat = (
        jnp.einsum("hfd,thd->thf", prev_state, d_numer, precision=HIGH)
        + prev_norm[None] * d_denom[:, :, None]
    )
    d_kfeat = jnp.einsum("hfd,shd->shf", next_state, value_f32, precision=HIGH) + next_norm[None]
    d_query = (
        jnp.einsum("hts,shf->thf", d_scores, lin_key, precision=HIGH) * inv_root
        + query_pull(d_qfeat)[0]
    )
    d_key = (
        jnp.einsum("hts,thf->shf", d_scores, lin_query, precision=HIGH) * inv_root
        + key_pull(d_kfeat)[0]
    )
    return (d_query, d_key, d_values)


def window_block(query, key_rows, value_rows, grads, start):
    q_count = query.shape[0]
    k_count = key_rows.shape[0]
    inv_root = 1.0 / math.sqrt(query.shape[2])
    query_pos = start + jnp.arange(q_count, dtype=jnp.int32)[:, None]
    key_pos = start - (k_count - q_count) + jnp.arange(k_count, dtype=jnp.int32)[None, :]
    allowed = (key_pos <= query_pos) & (key_pos > query_pos - WINDOW) & (key_pos >= 0)
    logits = (
        jnp.einsum("thd,shd->hts", query, key_rows, preferred_element_type=jnp.float32) * inv_root
    )
    logits = jnp.where(allowed[None], logits, -1e30)
    shifted = jnp.exp(logits - jnp.max(logits, -1, keepdims=True))
    attn_weights = shifted / jnp.sum(shifted, -1, keepdims=True)
    attn_low = attn_weights.astype(jnp.bfloat16)
    result = jnp.einsum("hts,shd->thd", attn_low, value_rows, preferred_element_type=jnp.float32)
    d_attn = jnp.einsum("thd,shd->hts", grads, value_rows, preferred_element_type=jnp.float32)
    d_values = jnp.einsum("hts,thd->shd", attn_low, grads, preferred_element_type=jnp.float32)
    row_inner = jnp.sum(grads.astype(jnp.float32) * result, -1).T
    d_logits = (attn_weights * (d_attn - row_inner[:, :, None])).astype(jnp.bfloat16)
    d_query = (
        jnp.einsum("hts,shd->thd", d_logits, key_rows, preferred_element_type=jnp.float32)
        * inv_root
    )
    d_keys = (
        jnp.einsum("hts,thd->shd", d_logits, query, preferred_element_type=jnp.float32) * inv_root
    )
    return (result, d_query, d_keys, d_values)


def add_pair(earlier, later):
    return (earlier[0] + later[0], earlier[1] + later[1])


def local(q_lin, k_lin, q_win, k_win, values, grad_out):
    tokens_here = q_lin.shape[0]
    offset = lax.axis_index("seq") * tokens_here
    head_group = min(4, H)
    row_width = H * DH
    query_low = q_lin.reshape(tokens_here, H, FD)
    key_low = k_lin.reshape(tokens_here, H, FD)
    lin_query = query_low.astype(jnp.float32)
    lin_key = key_low.astype(jnp.float32)
    value_f32 = values.reshape(tokens_here, H, DH).astype(jnp.float32)
    grad_f32 = grad_out.reshape(tokens_here, H, DH).astype(jnp.float32)
    key_feat, key_pull = jax.vjp(feat_full, lin_key)
    own_state = jnp.einsum("thf,thd->hfd", key_feat, value_f32, precision=HIGH)
    own_norm = jnp.sum(key_feat, 0)
    prev_state, prev_norm = carried_in(
        (own_state, own_norm),
        "seq",
        add_pair,
        (jnp.zeros_like(own_state), jnp.zeros_like(own_norm)),
        False,
    )
    tail_rows = jnp.stack([k_win, values])
    before = passed_along(tail_rows, "seq", 1)
    key_rows = jnp.concatenate([before[0], k_win], 0)
    value_rows = jnp.concatenate([before[1], values], 0)
    block_results = []
    for head_first in range(0, H, head_group):
        columns = slice(head_first * DH, (head_first + head_group) * DH)
        block_results.append(
            window_block(
                q_win[:, columns].reshape(tokens_here, head_group, DH),
                key_rows[:, columns].reshape(tokens_here + WINDOW, head_group, DH),
                value_rows[:, columns].reshape(tokens_here + WINDOW, head_group, DH),
                grad_out[:, columns].reshape(tokens_here, head_group, DH),
                offset,
            )
        )
    win_out = jnp.concatenate(
        [entry[0].reshape(tokens_here, head_group * DH) for entry in block_results], 1
    )
    win_dq = jnp.concatenate(
        [entry[1].reshape(tokens_here, head_group * DH) for entry in block_results], 1
    )
    win_dk = jnp.concatenate(
        [entry[2].reshape(tokens_here + WINDOW, head_group * DH) for entry in block_results], 1
    )
    win_dv = jnp.concatenate(
        [entry[3].reshape(tokens_here + WINDOW, head_group * DH) for entry in block_results], 1
    )
    returned = passed_along(
        jnp.stack([win_dk[:WINDOW], win_dv[:WINDOW]]).astype(jnp.bfloat16), "seq", -1
    ).astype(jnp.float32)
    filler = jnp.zeros((tokens_here - WINDOW, row_width), jnp.float32)
    grad_k_win = (win_dk[WINDOW:] + jnp.concatenate([filler, returned[0]], 0)).astype(jnp.bfloat16)
    win_dv_own = win_dv[WINDOW:] + jnp.concatenate([filler, returned[1]], 0)
    query_feat, query_pull = jax.vjp(feat_full, lin_query)
    scores, kernel, causal = linear_pieces(query_low, key_low)
    numer = jnp.einsum("thf,hfd->thd", query_feat, prev_state, precision=HIGH) + jnp.einsum(
        "hts,shd->thd", kernel, value_f32, precision=HIGH
    )
    denom = jnp.einsum("thf,hf->th", query_feat, prev_norm, precision=HIGH) + jnp.sum(kernel, -1).T
    lin_out = numer / denom[:, :, None]
    mixed = (lin_out.reshape(tokens_here, row_width) + win_out).astype(jnp.bfloat16)
    d_numer = grad_f32 / denom[:, :, None]
    d_denom = -jnp.sum(grad_f32 * lin_out, -1) / denom
    own_back = jnp.einsum("thf,thd->hfd", query_feat, d_numer, precision=HIGH)
    own_back_norm = jnp.einsum("thf,th->hf", query_feat, d_denom, precision=HIGH)
    next_state, next_norm = carried_in(
        (own_back, own_back_norm),
        "seq",
        add_pair,
        (jnp.zeros_like(own_back), jnp.zeros_like(own_back_norm)),
        True,
    )
    lin_dq, lin_dk, lin_dv = linear_grads(
        lin_query,
        lin_key,
        value_f32,
        d_numer,
        d_denom,
        prev_state,
        prev_norm,
        next_state,
        next_norm,
        scores,
        kernel,
        causal,
        key_feat,
        query_pull,
        key_pull,
    )
    grad_q_lin = lin_dq.reshape(tokens_here, H * FD).astype(jnp.bfloat16)
    grad_k_lin = lin_dk.reshape(tokens_here, H * FD).astype(jnp.bfloat16)
    grad_q_win = win_dq.astype(jnp.bfloat16)
    grad_values = (lin_dv.reshape(tokens_here, row_width) + win_dv_own).astype(jnp.bfloat16)
    return (mixed, grad_q_lin, grad_k_lin, grad_q_win, grad_k_win, grad_values)


def solution(mesh):
    placed = (
        P(("dp", "seq"), None),
        P(("dp", "seq"), None),
        P(("dp", "seq"), None),
        P(("dp", "seq"), None),
        P(("dp", "seq"), None),
        P(("dp", "seq"), None),
    )
    return jax.shard_map(
        local,
        mesh=mesh,
        in_specs=placed,
        out_specs=(
            P(("dp", "seq"), None),
            P(("dp", "seq"), None),
            P(("dp", "seq"), None),
            P(("dp", "seq"), None),
            P(("dp", "seq"), None),
            P(("dp", "seq"), None),
        ),
        check_vma=False,
    )
```

profile of v0, /device:TPU:6, one launch (start us, length us, event | category | flops | bytes accessed | tf_op | source)
XLA Modules:
  0.0 1268.2 jit_solution(10875303684952757782)
XLA Ops:
  13.7 58.8 %all-gather.1 = f32[512,273]{1,0:T(8,128)} all-gather(f32[16,273]{1,0:T(8,128)S(1)} %fusion.11), channel_id=3, replica_groups=mesh['dp'=8,'seq'=32] {'seq'}, dimensions={0}, use_global_device_ids=true | all-gather | bytes 576576 | tf_op jit(solution)/shard_map/all_gather | solution.py:21
  75.6 276.1 %all-gather.7.cloned.1.call-done = f32[512,273,64]{1,2,0:T(8,128)} async-done(((f32[16,273,64]{1,2,0:T(8,128)}), f32[512,273,64]{1,2,0:T(8,128)}) %all-gather.7.cloned.1.call-update) | async-done | bytes 35782672 | tf_op jit(solution)/shard_map/all_gather | solution.py:21
  358.8 10.6 collective-permute-start
  371.9 8.1 collective-permute-done
  409.6 18.5 %collective-permute-done.1 = bf16[2,128,1024]{2,1,0:T(8,128)(2,1)} collective-permute-done((bf16[2,128,1024]{2,1,0:T(8,128)(2,1)}, bf16[2,128,1024]{2,1,0:T(8,128)(2,1)}, u32[]{:S(2)}, u32[]{:S(2)}) %collective-permute-start.1) | collective-permute-done | bytes 524320 | tf_op jit(solution)/shard_map/ppermute | solution.py:36
  429.2 4.0 convolution_bitcast_fusion.1
  446.5 319.7 %all-gather.3 = f32[512,273]{1,0:T(8,128)} all-gather(f32[16,273]{1,0:T(8,128)S(1)} %bitcast.399), channel_id=5, replica_groups=mesh['dp'=8,'seq'=32] {'seq'}, dimensions={0}, use_global_device_ids=true | all-gather | bytes 576576 | tf_op jit(solution)/shard_map/all_gather | solution.py:21
  768.0 202.8 %all-gather.9.cloned.1.call-done = f32[512,273,64]{1,2,0:T(8,128)} async-done(((f32[16,273,64]{1,2,0:T(8,128)}), f32[512,273,64]{1,2,0:T(8,128)}) %all-gather.9.cloned.1.call-update) | async-done | bytes 35782672 | tf_op jit(solution)/shard_map/all_gather | solution.py:21
  972.4 271.4 %while.27 = (s32[]{:T(128)}, f32[16,273,64]{2,1,0:T(8,128)}, f32[16,273]{1,0:T(8,128)S(1)}, s32[]{:T(128)}, f32[32,16,273,64]{2,3,1,0:T(8,128)}, /*index=5*/f32[...) while((s32[]{:T(128)}, f32[16,273,64]{2,1,0:T(8,128)}, f32[16,273]{1,0:T(8,128)S(1)}, ...), condition=%wide.region_16.17_spmd, body=%wide.region_15.16_spmd.sunk | while | flops 283926 | bytes 7880035 | solution.py:30
  977.1 3.3 bitcast_add_fusion.11
  985.9 3.3 bitcast_add_fusion.11
  994.6 3.3 bitcast_add_fusion.11
  1003.4 3.3 bitcast_add_fusion.11
  1012.1 3.3 bitcast_add_fusion.11
  1020.9 3.3 bitcast_add_fusion.11
  1029.6 3.3 bitcast_add_fusion.11
  1038.4 3.3 bitcast_add_fusion.11
  1047.1 3.3 bitcast_add_fusion.11
  1055.9 3.3 bitcast_add_fusion.11
  1064.6 3.3 bitcast_add_fusion.11
  1073.4 3.3 bitcast_add_fusion.11
  1082.1 3.3 bitcast_add_fusion.11
  1108.4 3.3 bitcast_add_fusion.11
  1117.2 3.3 bitcast_add_fusion.11
  1152.2 3.3 bitcast_add_fusion.11
  1160.9 3.3 bitcast_add_fusion.11
  1195.9 3.3 bitcast_add_fusion.11
  1204.7 3.3 bitcast_add_fusion.11
  1231.0 3.3 bitcast_add_fusion.11
  1239.7 3.3 bitcast_add_fusion.11
  1243.8 5.5 fusion.10
  1253.8 3.6 convolution_add_fusion.1
  (350 shorter events, 275.1 us)
Async XLA Ops:
  7.2 344.5 %all-gather.7.cloned.1.call-start = ((), (), s32[]{:S(2)}) async-start(), calls=%async_computation | async-start | bytes 51904512 | tf_op jit(solution)/shard_map/all_gather | solution.py:21
  8.2 64.4 %copy-start.24 = (bf16[128,256]{0,1:T(8,128)(2,1)}, bf16[128,256]{0,1:T(8,128)(2,1)S(1)}, u32[]{:S(2)}) copy-start(bf16[128,256]{0,1:T(8,128)(2,1)S(1)} %copy.149) | copy-start | bytes 196612
  8.2 4.4 copy-start.17
  12.2 958.6 %all-gather.9.cloned.1.call-start = ((), (), s32[]{:S(2)}) async-start(), calls=%async_computation.1 | async-start | bytes 51904512 | tf_op jit(solution)/shard_map/all_gather | solution.py:21
  12.4 343.4 %copy-start.18 = (f32[128,1024]{0,1:T(8,128)}, f32[128,1024]{0,1:T(8,128)S(1)}, u32[]{:S(2)}) copy-start(f32[128,1024]{0,1:T(8,128)S(1)} %copy.176) | copy-start | bytes 1572868
  12.6 61.4 %copy-start.22 = (bf16[128,256]{0,1:T(8,128)(2,1)}, bf16[128,256]{0,1:T(8,128)(2,1)S(1)}, u32[]{:S(2)}) copy-start(bf16[128,256]{0,1:T(8,128)(2,1)S(1)} %copy.152) | copy-start | bytes 196612
  12.6 61.4 %copy-start.53 = (pred[128,128]{0,1:T(8,128)(4,1)}, pred[128,128]{0,1:T(8,128)(4,1)S(1)}, u32[]{:S(2)}) copy-start(pred[128,128]{0,1:T(8,128)(4,1)S(1)} %iota_compare_fusion) | copy-start | bytes 49156
  72.6 283.2 %copy-start.28 = (f32[128,16,16]{0,2,1:T(8,128)}, f32[128,16,16]{0,2,1:T(8,128)S(1)}, u32[]{:S(2)}) copy-start(f32[128,16,16]{0,2,1:T(8,128)S(1)} %broadcast_multiply_fusion) | copy-start | bytes 393220
  358.7 10.9 copy-start.50
  358.8 21.2 %collective-permute-start = (bf16[2,128,1024]{2,1,0:T(8,128)(2,1)S(1)}, bf16[2,128,1024]{2,1,0:T(8,128)(2,1)S(1)}, u32[]{:S(2)}, u32[]{:S(2)}) collective-permute-start(bf16[2,128,1024]{2,1,0:T(8,128)(2,1)S(1)} %pad_maximum_fusion.6), channel_id=1, source_target_pairs={{0,1},{1,2},{2,3},{3,4},{4,5},{5,6},{6,7},{7,8},{8,9},{9,10},{10,1... | collective-permute-start | bytes 1572872 | tf_op jit(solution)/shard_map/ppermute | solution.py:36
  369.8 12.3 copy-start.46
  371.7 18.5 %copy-start.43 = (bf16[128,256]{0,1:T(8,128)(2,1)}, bf16[128,256]{0,1:T(8,128)(2,1)S(1)}, u32[]{:S(2)}) copy-start(bf16[128,256]{0,1:T(8,128)(2,1)S(1)} %copy.157) | copy-start | bytes 196612
  386.0 4.6 copy-start.37
  386.1 4.6 copy-start.30
  386.6 4.1 copy-start.33
  390.7 5.6 copy-start.35
  390.7 4.2 copy-start.58
  390.7 4.2 copy-start.59
  390.8 4.1 copy-start.42
  403.9 25.3 %copy-start.1 = (f32[16,273,64]{2,1,0:T(8,128)S(1)}, f32[16,273,64]{2,1,0:T(8,128)}, u32[]{:S(2)}) copy-start(f32[16,273,64]{2,1,0:T(8,128)} %get-tuple-element.121) | copy-start | bytes 3354628
  404.8 23.2 %collective-permute-start.1 = (bf16[2,128,1024]{2,1,0:T(8,128)(2,1)}, bf16[2,128,1024]{2,1,0:T(8,128)(2,1)}, u32[]{:S(2)}, u32[]{:S(2)}) collective-permute-start(bf16[2,128,1024]{2,1,0:T(8,128)(2,1)} %pad_maximum_fusion.7), channel_id=1, source_target_pairs={{1,0},{2,1},{3,2},{4,3},{5,4},{6,5},{7,6},{8,7},{9,8},{10,9},{11,1... | collective-permute-start | bytes 1572872 | tf_op jit(solution)/shard_map/ppermute | solution.py:36
  429.2 4.1 copy-start.14
  429.2 4.1 copy-start.19
  429.2 4.1 copy-start.54
  436.8 4.3 copy-start.52
  438.9 4.2 copy-start.5
  443.1 323.0 %copy-start.29 = (f32[128,256]{1,0:T(8,128)S(1)}, f32[128,256]{1,0:T(8,128)}, u32[]{:S(2)}) copy-start(f32[128,256]{1,0:T(8,128)} %copy.174) | copy-start | bytes 393220
  444.2 321.9 %copy-start.21 = (f32[128,1024]{1,0:T(8,128)S(1)}, f32[128,1024]{1,0:T(8,128)}, u32[]{:S(2)}) copy-start(f32[128,1024]{1,0:T(8,128)} %copy.175) | copy-start | bytes 1572868
  1243.8 5.5 copy-start
  1243.8 5.5 copy-start.15
  1253.8 5.6 copy-start.10
  1253.8 5.6 copy-start.12
  (33 other events, 79.4 us)
Sparse Core Ops, SparseCore 0:
  12.3 339.2 all-gather.6
  358.9 611.8 all-gather.8
where the time goes:
time: 1270 us
  waiting for transfers between devices  506 us (40%)
  blocking collectives  378 us (30%)
  local copies, waits for them, and re-layouts  170 us (13%)
  other arithmetic  141 us (11%)
  matrix products  45.7 us (4%)
  between operations  15.4 us (1%)
    all_gather x2, waiting for transfers between devices, carried_in(): gathered = jax.tree.map(lambda a: lax.all_gather(a, axis), part)  479 us
    all_gather x2, blocking collectives, carried_in(): gathered = jax.tree.map(lambda a: lax.all_gather(a, axis), part)  378 us
    dynamic_slice x62, local copies, waits for them, and re-layouts, one(): lax.dynamic_index_in_dim(a, source, 0, False)  145 us
    add x62, other arithmetic, add_pair(): return (earlier[0] + later[0], earlier[1] + later[1])  126 us
    ppermute x2, waiting for transfers between devices, passed_along(): lax.ppermute(value, axis, [(source, source + steps) for source in range(l...  26.6 us
  transfers between devices with their start and end apart: 4, of which 4 were waited for; matrix products, arithmetic and copies ran while one was open for 4% of the time, Pallas kernels for 0%

commit v1 on v0

v1 whole, which is shorter than its diff:
```python
import functools

import jax
import jax.numpy as jnp
from jax import lax
from jax.experimental import pallas as pl
from jax.experimental.pallas import tpu as pltpu
from jax.sharding import Mesh, PartitionSpec as P

H = 16
DH = 64
FD = 16
TOK = 128
FEAT = 224
ROWS = 80
WIDE = 256
STEPS = 8
BF = jnp.bfloat16
F32 = jnp.float32
PARAMS = pltpu.CompilerParams(vmem_limit_bytes=16 * 1024 * 1024)


def nn(a, b):
    return lax.dot_general(a, b, (((1,), (0,)), ((), ())), preferred_element_type=F32)


def nt(a, b):
    return lax.dot_general(a, b, (((1,), (1,)), ((), ())), preferred_element_type=F32)


def split(x):
    high = x.astype(BF)
    return high, (x - high.astype(F32)).astype(BF)


def flip(x):
    return jnp.transpose(x.astype(F32)).astype(BF)


def pack_kernel(
    ql_hbm, kl_hbm, kw_hbm, v_hbm, g_hbm, out_ref, halo_hbm,
    ql_ref, kl_ref, kw_ref, v_ref, g_ref, sems,
):
    def copy(source, target, i):
        job = pltpu.make_async_copy(source, target, sems.at[i])
        job.start()
        return job

    value_in = copy(v_hbm, v_ref, 0)
    window_in = copy(kw_hbm, kw_ref, 1)
    grad_in = copy(g_hbm, g_ref, 2)
    key_in = copy(kl_hbm, kl_ref, 3)
    query_in = copy(ql_hbm, ql_ref, 4)
    value_in.wait()
    value_out = copy(v_ref, halo_hbm.at[1], 5)
    window_in.wait()
    window_out = copy(kw_ref, halo_hbm.at[0], 6)

    def wide(ref, base):
        for p in range(8):
            part = flip(ref[:, p * 128 : (p + 1) * 128])
            out_ref[2 * p, base : base + 64, :] = part[0:64]
            out_ref[2 * p + 1, base : base + 64, :] = part[64:128]

    def thin(ref, base):
        for j in range(2):
            part = flip(ref[:, j * 128 : (j + 1) * 128])
            for i in range(8):
                out_ref[8 * j + i, base : base + 16, :] = part[16 * i : 16 * i + 16]

    wide(v_ref, 16)
    grad_in.wait()
    wide(g_ref, 96)
    key_in.wait()
    thin(kl_ref, 0)
    query_in.wait()
    thin(ql_ref, 80)
    value_out.wait()
    window_out.wait()


def pack(q_lin, k_lin, k_win, values, grad_out):
    hbm = pl.BlockSpec(memory_space=pltpu.HBM)
    return pl.pallas_call(
        pack_kernel,
        in_specs=[hbm] * 5,
        out_specs=(pl.BlockSpec(memory_space=pltpu.VMEM), hbm),
        out_shape=(
            jax.ShapeDtypeStruct((H, 2 * ROWS, TOK), BF),
            jax.ShapeDtypeStruct((2, TOK, H * DH), BF),
        ),
        scratch_shapes=[
            pltpu.VMEM((TOK, H * FD), BF),
            pltpu.VMEM((TOK, H * FD), BF),
            pltpu.VMEM((TOK, H * DH), BF),
            pltpu.VMEM((TOK, H * DH), BF),
            pltpu.VMEM((TOK, H * DH), BF),
            pltpu.SemaphoreType.DMA((7,)),
        ],
        compiler_params=pltpu.CompilerParams(vmem_limit_bytes=60 * 1024 * 1024),
        name="pack",
    )(q_lin, k_lin, k_win, values, grad_out)


def features(x, square=1.0, cross=1.0, linear=1.0):
    low, up = x[0:8], x[8:16]
    left, mix, right = low * square, up * cross, up * square
    pieces = []
    for i in range(8):
        row = x[i : i + 1]
        pieces += [row * left, row * mix]
    for i in range(8, 16):
        pieces.append(x[i : i + 1] * right)
    pieces += [low * linear, up * linear]
    one = (lax.broadcasted_iota(jnp.int32, (8, x.shape[1]), 0) == 0).astype(F32)
    pieces += [one, jnp.zeros_like(one)]
    return jnp.concatenate(pieces, 0).astype(BF)


def pull(x, grad, weight):
    low, up = x[0:8], x[8:16]
    row_id = lax.broadcasted_iota(jnp.int32, low.shape, 0)
    acc_low = jnp.zeros_like(low)
    acc_mix = jnp.zeros_like(low)
    acc_up = jnp.zeros_like(low)
    red = jnp.zeros_like(low)
    for i in range(8):
        row = x[i : i + 1]
        own = grad[16 * i : 16 * i + 8]
        mix = grad[16 * i + 8 : 16 * i + 16]
        acc_low = acc_low + row * own
        acc_mix = acc_mix + row * mix
        red = jnp.where(row_id == i, jnp.sum(up * mix, 0, keepdims=True), red)
    for i in range(8, 16):
        acc_up = acc_up + x[i : i + 1] * grad[128 + 8 * (i - 8) : 136 + 8 * (i - 8)]
    if weight:
        out_low = (acc_low + red) * (1.0 / 16.0) + grad[192:200] * 0.25
        out_up = (acc_mix + acc_up) * (1.0 / 16.0) + grad[200:208] * 0.25
    else:
        out_low = 2.0 * acc_low + red + grad[192:200]
        out_up = acc_mix + 2.0 * acc_up + grad[200:208]
    return jnp.concatenate([out_low, out_up], 0)


def rows_of(ref, c, start, stop):
    return jnp.concatenate([ref[2 * c, start:stop], ref[2 * c + 1, start:stop]], 1)


def with_ones(v):
    tail = (lax.broadcasted_iota(jnp.int32, (16, v.shape[1]), 0) == 0).astype(BF)
    return jnp.concatenate([v, tail], 0)


def state_kernel(x_ref, pref_ref, total_ref, feat_ref):
    run = jnp.zeros((ROWS, FEAT), F32)
    for c in range(STEPS):
        pref_ref[c] = run
        key = rows_of(x_ref, c, 0, 16).astype(F32)
        feat = features(key, 1.0 / 32.0, 1.0 / 16.0, 0.25)
        feat_ref[c] = feat
        ones = with_ones(rows_of(x_ref, c, 16, 80))
        run = run + nt(ones, feat)
    total_ref[...] = run


def key_state(x):
    feat = jax.ShapeDtypeStruct((STEPS, FEAT, WIDE), BF)
    return pl.pallas_call(
        state_kernel,
        out_shape=(
            jax.ShapeDtypeStruct((STEPS, ROWS, FEAT), F32),
            jax.ShapeDtypeStruct((ROWS, FEAT), F32),
            feat,
        ),
        compiler_params=PARAMS,
        name="key_state",
    )(x)


def causal_mask():
    source = lax.broadcasted_iota(jnp.int32, (WIDE, WIDE), 0)
    target = lax.broadcasted_iota(jnp.int32, (WIDE, WIDE), 1)
    return source <= target


def inside_kernel(x_ref, scores_ref, numer_ref, feat_ref):
    causal = causal_mask()
    for c in range(STEPS):
        key = rows_of(x_ref, c, 0, 16)
        query = rows_of(x_ref, c, 80, 96)
        ones = with_ones(rows_of(x_ref, c, 16, 80))
        scores = nn(flip(key), query) * 0.25
        scores_ref[c] = scores
        kernel_hi, kernel_lo = split(
            jnp.where(causal, 1.0 + scores + 0.5 * scores * scores, 0.0)
        )
        numer_ref[c] = nn(ones, kernel_hi) + nn(ones, kernel_lo)
        feat_ref[c] = features(query.astype(F32))


def inside(x):
    feat = jax.ShapeDtypeStruct((STEPS, FEAT, WIDE), BF)
    return pl.pallas_call(
        inside_kernel,
        out_shape=(
            jax.ShapeDtypeStruct((STEPS, WIDE, WIDE), F32),
            jax.ShapeDtypeStruct((STEPS, ROWS, WIDE), F32),
            feat,
        ),
        compiler_params=PARAMS,
        name="inside_chunks",
    )(x)


def output_kernel(
    x_ref, pref_ref, half_ref, numer_ref, feat_ref,
    lin_ref, dhi_ref, dlo_ref, own_ref, total_ref,
):
    total = jnp.zeros((ROWS, FEAT), F32)
    first = lax.broadcasted_iota(jnp.int32, (16, WIDE), 0) == 0
    for c in range(STEPS):
        grads = rows_of(x_ref, c, 96, 160).astype(F32)
        feat = feat_ref[c]
        state_hi, state_lo = split(pref_ref[c] + half_ref[...])
        stack = nn(jnp.concatenate([state_hi, state_lo], 0), feat)
        numer = numer_ref[c] + stack[0:ROWS] + stack[ROWS:]
        inv = 1.0 / numer[64:65]
        lin_out = numer[0:64] * inv
        d_denom = -jnp.sum(grads * lin_out, 0, keepdims=True) * inv
        d_hi, d_lo = split(
            jnp.concatenate([grads * inv, jnp.where(first, d_denom, 0.0)], 0)
        )
        stack = nt(jnp.concatenate([d_hi, d_lo], 0), feat)
        own = stack[0:ROWS] + stack[ROWS:]
        own_ref[c] = own
        total = total + own
        lin_ref[c] = lin_out.astype(BF)
        dhi_ref[c] = d_hi
        dlo_ref[c] = d_lo
    total_ref[...] = total


def output(x, pref, half, numer, feat):
    side = jax.ShapeDtypeStruct((STEPS, ROWS, WIDE), BF)
    return pl.pallas_call(
        output_kernel,
        out_shape=(
            jax.ShapeDtypeStruct((STEPS, DH, WIDE), BF),
            side,
            side,
            jax.ShapeDtypeStruct((STEPS, ROWS, FEAT), F32),
            jax.ShapeDtypeStruct((ROWS, FEAT), F32),
        ),
        compiler_params=PARAMS,
        name="linear_output",
    )(x, pref, half, numer, feat)


def query_kernel(x_ref, scores_ref, pref_ref, half_ref, dhi_ref, dlo_ref, dq_ref, part_ref):
    causal = causal_mask()
    for c in range(STEPS):
        key = rows_of(x_ref, c, 0, 16)
        query = rows_of(x_ref, c, 80, 96)
        ones_t = flip(with_ones(rows_of(x_ref, c, 16, 80)))
        d_hi, d_lo = dhi_ref[c], dlo_ref[c]
        scores = scores_ref[c]
        kernel = jnp.where(causal, 1.0 + scores + 0.5 * scores * scores, 0.0).astype(BF)
        turned_hi, turned_lo = split(jnp.transpose(pref_ref[c] + half_ref[...]))
        d_feat = nn(turned_hi, d_hi) + nn(turned_lo, d_hi) + nn(turned_hi, d_lo)
        d_kernel = nn(ones_t, d_hi) + nn(ones_t, d_lo)
        d_scores = jnp.where(causal, d_kernel * (1.0 + scores), 0.0).astype(BF)
        d_query = pull(query.astype(F32), d_feat, False) + nn(key, d_scores) * 0.25
        dq_ref[c] = d_query.astype(BF)
        part_ref[c, 0:64] = nt(d_hi[0:64], kernel)
        part_ref[c, 64:80] = nt(query, d_scores) * 0.25


def query_grads(x, scores, pref, half, d_hi, d_lo):
    return pl.pallas_call(
        query_kernel,
        out_shape=(
            jax.ShapeDtypeStruct((STEPS, FD, WIDE), BF),
            jax.ShapeDtypeStruct((STEPS, ROWS, WIDE), F32),
        ),
        compiler_params=PARAMS,
        name="query_grads",
    )(x, scores, pref, half, d_hi, d_lo)


def key_kernel(x_ref, lin_ref, dq_ref, part_ref, own_ref, half_ref, feat_ref, out_ref):
    run = half_ref[...]
    for c in range(STEPS - 1, -1, -1):
        key = rows_of(x_ref, c, 0, 16).astype(F32)
        ones = with_ones(rows_of(x_ref, c, 16, 80))
        feat = feat_ref[c]
        run_hi, run_lo = split(run)
        stack = nn(jnp.concatenate([run_hi[0:64], run_lo[0:64]], 0), feat)
        d_value = stack[0:64] + stack[64:128] + part_ref[c, 0:64]
        turned_hi, turned_lo = split(jnp.transpose(run))
        d_feat = nn(turned_hi, ones) + nn(turned_lo, ones)
        d_key = (pull(key, d_feat, True) + part_ref[c, 64:80]).astype(BF)
        d_value = d_value.astype(BF)
        for i in range(2):
            cols = slice(i * TOK, (i + 1) * TOK)
            out_ref[2 * c + i, 0:64] = lin_ref[c, :, cols]
            out_ref[2 * c + i, 64:80] = dq_ref[c, :, cols]
            out_ref[2 * c + i, 80:144] = d_value[:, cols]
            out_ref[2 * c + i, 144:160] = d_key[:, cols]
        if c:
            run = run + own_ref[c]


def key_grads(x, lin, dq, part, own, half, feat):
    return pl.pallas_call(
        key_kernel,
        out_shape=jax.ShapeDtypeStruct((H, 2 * ROWS, TOK), BF),
        compiler_params=PARAMS,
        name="key_grads",
    )(x, lin, dq, part, own, half, feat)


def window_kernel(
    first_ref, q_ref, k_ref, v_ref, g_ref, halo_ref,
    out_ref, dq_ref, dk_ref, dv_ref, back_hbm, back_ref, sems,
):
    source = lax.broadcasted_iota(jnp.int32, (TOK, 2 * TOK), 0)
    target = lax.broadcasted_iota(jnp.int32, (TOK, 2 * TOK), 1) % TOK
    own = source <= target
    own_low = own.astype(F32).astype(BF)
    prev_low = (1.0 - own.astype(F32)).astype(BF)
    row = lax.broadcasted_iota(jnp.int32, (TOK, TOK), 0)
    col = lax.broadcasted_iota(jnp.int32, (TOK, TOK), 1)
    own_t = (col <= row).astype(F32).astype(BF)
    prev_t = (col > row).astype(F32).astype(BF)
    lane_a = (col < DH).astype(F32).astype(BF)
    lane_b = (col >= DH).astype(F32).astype(BF)
    blocked = jnp.where(first_ref[0] == 1, -1e30, 0.0)

    def both(x):
        return jnp.concatenate([x * lane_a, x * lane_b], 0)

    copies = []
    for p in range(H // 2):
        cols = slice(p * 128, (p + 1) * 128)
        key, key_p = k_ref[:, cols], halo_ref[0, :, cols]
        value, value_p = v_ref[:, cols], halo_ref[1, :, cols]
        query2 = both(q_ref[:, cols])
        grad2 = both(g_ref[:, cols])
        logits = jnp.where(own, nt(key, query2) * 0.125, nt(key_p, query2) * 0.125 + blocked)
        shifted = jnp.exp(logits - jnp.max(logits, 0, keepdims=True))
        attn = shifted * (1.0 / jnp.sum(shifted, 0, keepdims=True))
        attn_low = attn.astype(BF)
        pieces = []
        for i in range(2):
            turned = flip(attn_low[:, i * TOK : (i + 1) * TOK])
            pieces += [turned * own_t, turned * prev_t]
        values4 = jnp.concatenate(
            [value * lane_a, value_p * lane_a, value * lane_b, value_p * lane_b], 0
        )
        result = nn(jnp.concatenate(pieces, 1), values4)
        out_ref[:, cols] = result
        inner_t = jnp.transpose(result * g_ref[:, cols].astype(F32))
        inner = jnp.concatenate(
            [jnp.sum(inner_t[0:64], 0, keepdims=True), jnp.sum(inner_t[64:128], 0, keepdims=True)],
            1,
        )
        d_attn = jnp.where(own, nt(value, grad2), nt(value_p, grad2))
        d_logits = (attn * (d_attn - inner)).astype(BF)
        pieces = []
        for i in range(2):
            turned = flip(d_logits[:, i * TOK : (i + 1) * TOK])
            pieces += [turned * own_t, turned * prev_t]
        keys4 = jnp.concatenate([key * lane_a, key_p * lane_a, key * lane_b, key_p * lane_b], 0)
        dq_ref[:, cols] = (nn(jnp.concatenate(pieces, 1), keys4) * 0.125).astype(BF)
        dk_ref[:, cols] = nn(d_logits * own_low, query2) * 0.125
        back_ref[0, :, cols] = (nn(d_logits * prev_low, query2) * 0.125).astype(BF)
        dv_ref[:, cols] = nn(attn_low * own_low, grad2)
        back_ref[1, :, cols] = nn(attn_low * prev_low, grad2).astype(BF)
        copies.append(
            pltpu.make_async_copy(back_ref.at[:, :, cols], back_hbm.at[:, :, cols], sems.at[p])
        )
        copies[-1].start()
    for copy in copies:
        copy.wait()


def window(first, q, k, v, g, halo):
    wide = (TOK, H * DH)
    vmem = pl.BlockSpec(memory_space=pltpu.VMEM)
    return pl.pallas_call(
        window_kernel,
        in_specs=[pl.BlockSpec(memory_space=pltpu.SMEM)] + [vmem] * 5,
        out_specs=(vmem,) * 4 + (pl.BlockSpec(memory_space=pltpu.HBM),),
        out_shape=(
            jax.ShapeDtypeStruct(wide, F32),
            jax.ShapeDtypeStruct(wide, BF),
            jax.ShapeDtypeStruct(wide, F32),
            jax.ShapeDtypeStruct(wide, F32),
            jax.ShapeDtypeStruct((2,) + wide, BF),
        ),
        scratch_shapes=[pltpu.VMEM((2,) + wide, BF), pltpu.SemaphoreType.DMA((8,))],
        compiler_params=PARAMS,
        cost_estimate=pl.CostEstimate(
            flops=50_000_000_000, transcendentals=0, bytes_accessed=6_000_000
        ),
        name="window",
    )(first, q, k, v, g, halo)


def finish_kernel(
    y_ref, out_ref, dk_ref, dv_ref, halo_ref, mixed_ref, gq_ref, gk_ref, gkw_ref, gv_ref
):
    for p in range(8):
        cols = slice(p * 128, (p + 1) * 128)
        pair = jnp.concatenate([y_ref[2 * p, 0:64], y_ref[2 * p + 1, 0:64]], 0)
        mixed_ref[:, cols] = (jnp.transpose(pair.astype(F32)) + out_ref[:, cols]).astype(BF)
        pair = jnp.concatenate([y_ref[2 * p, 80:144], y_ref[2 * p + 1, 80:144]], 0)
        own = dv_ref[:, cols] + halo_ref[1, :, cols].astype(F32)
        gv_ref[:, cols] = (jnp.transpose(pair.astype(F32)) + own).astype(BF)
        gkw_ref[:, cols] = (dk_ref[:, cols] + halo_ref[0, :, cols].astype(F32)).astype(BF)
    for j in range(2):
        cols = slice(j * 128, (j + 1) * 128)
        for ref, row in ((gq_ref, 64), (gk_ref, 144)):
            ref[:, cols] = flip(
                jnp.concatenate([y_ref[8 * j + i, row : row + 16] for i in range(8)], 0)
            )


def finish(y, out, dk, dv, halo):
    wide = jax.ShapeDtypeStruct((TOK, H * DH), BF)
    thin = jax.ShapeDtypeStruct((TOK, H * FD), BF)
    return pl.pallas_call(
        finish_kernel,
        out_shape=(wide, thin, thin, wide, wide),
        compiler_params=PARAMS,
        name="finish",
    )(y, out, dk, dv, halo)


def local(q_lin, k_lin, q_win, k_win, values, grad_out):
    seq = ("half", "head")
    spread = functools.partial(
        lax.all_to_all, axis_name="head", split_axis=0, concat_axis=0, tiled=True
    )
    later = [(i, i + 1) for i in range(31)]
    earlier = [(i + 1, i) for i in range(31)]
    own, halo = pack(q_lin, k_lin, k_win, values, grad_out)
    halo = lax.ppermute(halo, seq, later)
    x = spread(own)
    first = (lax.axis_index(seq) == 0).astype(jnp.int32).reshape(1)
    out, dq_win, dk, dv, back_halo = window(first, q_win, k_win, values, grad_out, halo)
    back_halo = lax.ppermute(back_halo, seq, earlier)
    x, dk, dv = lax.optimization_barrier((x, dk, dv))
    pref, total, key_feat = key_state(x)
    half = lax.ppermute(total, "half", [(0, 1)])
    scores, numer, query_feat = inside(x)
    numer, half = lax.optimization_barrier((numer, half))
    lin, d_hi, d_lo, state, total = output(x, pref, half, numer, query_feat)
    next_half = lax.ppermute(total, "half", [(1, 0)])
    dq, part = query_grads(x, scores, pref, half, d_hi, d_lo)
    dq, back_halo = lax.optimization_barrier((dq, back_halo))
    y = spread(key_grads(x, lin, dq, part, state, next_half, key_feat))
    mixed, gq, gk, gkw, gv = finish(y, out, dk, dv, back_halo)
    return (mixed, gq, gk, dq_win, gkw, gv)


def solution(mesh):
    inner = Mesh(mesh.devices.reshape(8, 2, 16), ("dp", "half", "head"))
    placed = P(("dp", "half", "head"), None)
    return jax.shard_map(
        local, mesh=inner, in_specs=(placed,) * 6, out_specs=(placed,) * 6, check_vma=False
    )
```

time: 1270 us -> 85.3 us (0.07)
  waiting for transfers between devices: 506 us -> 15.9 us
  blocking collectives: 378 us -> 26.4 us
  local copies, waits for them, and re-layouts: 170 us -> 2.8 us
  other arithmetic: 141 us -> 0 us
  matrix products: 45.7 us -> 0 us
  Pallas kernels: 0 us -> 18.4 us
  between operations: 15.4 us -> 0.75 us
    all_gather x2 -> x0, waiting for transfers between devices: 479 us -> none  [carried_in(): gathered = jax.tree.map(lambda a: lax.all_gather(a, axis), part)]
    all_gather x2 -> x0, blocking collectives: 378 us -> none  [carried_in(): gathered = jax.tree.map(lambda a: lax.all_gather(a, axis), part)]
    dynamic_slice x62 -> x0, local copies, waits for them, and re-layouts: 145 us -> none  [one(): lax.dynamic_index_in_dim(a, source, 0, False)]
    add x65 -> x0, other arithmetic: 126 us -> none  [the longest x62 126 us: add_pair(): return (earlier[0] + later[0], earlier[1] + later[1])]
    dot_general x34 -> x0, matrix products: 44.1 us -> none  [the longest x1 5.54 us: linear_grads(): jnp.einsum('shf,hfd->shd', key_feat, next_state, precision=HIGH)]
    all_to_all x0 -> x1, blocking collectives: none -> 26.4 us  [local(): y = spread(key_grads(x, lin, dq, part, state, next_half, key_feat))]
    pallas_call x0 -> x8, Pallas kernels: none -> 18.4 us  [the longest x1 8.14 us: window(): pl.pallas_call(window_kernel, in_specs=[pl.BlockSpec(memory_space=pltpu.S...]
    ppermute x2 -> x4, waiting for transfers between devices: 26.6 us -> 8.48 us  [the longest x1 3.91 us: local(): halo = lax.ppermute(halo, seq, later)]
  transfers between devices with their start and end apart: 4 -> 5, of which waited for: 4 -> 4; matrix products, arithmetic and copies ran while one was open for 4% -> 0% of each run, Pallas kernels for 0% -> 16%
where the time goes in v1:
time: 85.3 us; the launch traced here: 84.9 us
  blocking collectives  26.4 us (31%)
  starting transfers between devices  20.7 us (24%)
  Pallas kernels  18.4 us (22%)
  waiting for transfers between devices  15.9 us (19%)
  local copies, waits for them, and re-layouts  2.8 us (3%)
    all_to_all x1, blocking collectives, local(): y = spread(key_grads(x, lin, dq, part, state, next_half, key_feat))  26.4 us
    all_to_all x1, starting transfers between devices, local(): x = spread(own)  8.67 us
    pallas_call x1, Pallas kernels, window(): pl.pallas_call(window_kernel, in_specs=[pl.BlockSpec(memory_space=pltpu.S...  8.14 us
    all_to_all x1, waiting for transfers between devices, local(): x = spread(own)  7.41 us
    ppermute x1, starting transfers between devices, local(): half = lax.ppermute(total, 'half', [(0, 1)])  5.58 us
    ppermute x1, waiting for transfers between devices, local(): halo = lax.ppermute(halo, seq, later)  3.91 us
    ppermute x1, starting transfers between devices, local(): halo = lax.ppermute(halo, seq, later)  3.85 us
    ppermute x1, waiting for transfers between devices, local(): next_half = lax.ppermute(total, 'half', [(1, 0)])  3.6 us
  transfers between devices with their start and end apart: 5, of which 4 were waited for; matrix products, arithmetic and copies ran while one was open for 0% of the time, Pallas kernels for 16%

profile of v1, /device:TPU:6, one launch (start us, length us, event | category | flops | bytes accessed | tf_op | source)
XLA Modules:
  0.0 84.9 jit_solution(5297997176073291694)
XLA Ops:
  0.6 0.0 copy-start.2
  0.6 0.0 copy-start.1
  0.7 0.0 copy-start
  0.7 2.7 %pack.1 = (bf16[16,160,128]{2,1,0:T(8,128)(2,1)}, bf16[2,128,1024]{2,1,0:T(8,128)(2,1)}) custom-call(bf16[128,256]{1,0:T(8,128)(2,1)} %ql_hbm.1, bf16[128,256]{1,0:T(8,128)(2,1)} %kl_hbm.1, bf16[128,1024]{1,0:T(8,128)(2,1)} %k_ref.1, bf16[128,1024]{1,0:T(8,128)(2,1)} %v_ref.1, bf16[128,1024]{1,0:T(8,128)(2,1)} %g_ref.1), custom_call_target="tpu_custom_call" | custom-call | tf_op jit(solution)/shard_map/pack/pallas_call | solution.py:84
  3.4 3.9 %collective-permute-start = (bf16[2,128,1024]{2,1,0:T(8,128)(2,1)}, bf16[2,128,1024]{2,1,0:T(8,128)(2,1)S(1)}, u32[]{:S(2)}, u32[]{:S(2)}) collective-permute-start(bf16[2,128,1024]{2,1,0:T(8,128)(2,1)} %get-tuple-element.39), channel_id=1, source_target_pairs={{0,1},{1,2},{2,3},{3,4},{4,5},{5,6},{6,7},{7,8},{8,9},{9,10},{10,1... | collective-permute-start | bytes 1572872 | tf_op jit(solution)/shard_map/ppermute | solution.py:448
  7.3 8.7 %all-to-all-start = ((bf16[16,160,128]{2,1,0:T(8,128)(2,1)}), bf16[16,160,128]{2,1,0:T(8,128)(2,1)S(1)}, u32[]{:S(2)}, u32[]{:S(2)}) async-start(bf16[16,160,128]{2,1,0:T(8,128)(2,1)} %get-tuple-element.38), calls=%async_computation | async-start | bytes 1310720 | tf_op jit(solution)/shard_map/all_to_all | solution.py:449
  15.9 3.9 %collective-permute-done.halo_ref = bf16[2,128,1024]{2,1,0:T(8,128)(2,1)S(1)} collective-permute-done((bf16[2,128,1024]{2,1,0:T(8,128)(2,1)}, bf16[2,128,1024]{2,1,0:T(8,128)(2,1)S(1)}, u32[]{:S(2)}, u32[]{:S(2)}) %collective-permute-start) | collective-permute-done | bytes 524320 | tf_op jit(solution)/shard_map/ppermute | solution.py:448
  19.9 0.0 copy-start.3
  19.9 0.8 copy-done.3
  20.7 0.0 copy-done.2
  20.7 0.0 copy-done.1
  20.7 0.0 copy-done
  20.7 0.0 copy-start.4
  20.7 1.0 %copy-done.4 = bf16[2,128,1024]{2,1,0:T(8,128)(2,1)S(1)} copy-done((bf16[2,128,1024]{2,1,0:T(8,128)(2,1)S(1)}, bf16[2,128,1024]{2,1,0:T(8,128)(2,1)}, u32[]{:S(2)}) %copy-start.4) | copy-done | bytes 524312
  21.7 0.0 copy-start.5
  21.7 0.9 %copy-done.5 = bf16[128,1024]{1,0:T(8,128)(2,1)S(1)} copy-done((bf16[128,1024]{1,0:T(8,128)(2,1)S(1)}, bf16[128,1024]{1,0:T(8,128)(2,1)}, u32[]{:S(2)}) %copy-start.5) | copy-done | bytes 262168
  22.7 8.1 %window.1 = (f32[128,1024]{1,0:T(8,128)S(1)}, bf16[128,1024]{1,0:T(8,128)(2,1)}, f32[128,1024]{1,0:T(8,128)S(1)}, f32[128,1024]{1,0:T(8,128)S(1)}, bf16[2,128,1024]{2,1,0:T(8,128)(2,1)S(1)}) custom-call(s32[1]{0:T(128)} %bitcast.first_ref, bf16[128,1024]{1,0:T(8,128)(2,1)S(1)} %copy-done.5, bf16[128,1024]{1,0:T(8,128)(2,1)S(1)} %copy-done, ...), custom_call_target="tpu_custom_call" | custom-call | flops 49999998976 | bytes 6000000 | tf_op jit(solution)/shard_map/window/pallas_call | solution.py:390
  30.8 1.3 %collective-permute-start.2 = (bf16[2,128,1024]{2,1,0:T(8,128)(2,1)S(1)}, bf16[2,128,1024]{2,1,0:T(8,128)(2,1)S(1)}, u32[]{:S(2)}, u32[]{:S(2)}) collective-permute-start(bf16[2,128,1024]{2,1,0:T(8,128)(2,1)S(1)} %get-tuple-element.54), channel_id=1, source_target_pairs={{1,0},{2,1},{3,2},{4,3},{5,4},{6,5},{7,6},{8,7},{9,8},{10,9},{11,1... | collective-permute-start | bytes 1572872 | tf_op jit(solution)/shard_map/ppermute | solution.py:452
  32.1 7.4 %all-to-all-done.x_ref = bf16[16,160,128]{2,1,0:T(8,128)(2,1)S(1)} async-done(((bf16[16,160,128]{2,1,0:T(8,128)(2,1)}), bf16[16,160,128]{2,1,0:T(8,128)(2,1)S(1)}, u32[]{:S(2)}, u32[]{:S(2)}) %all-to-all-start) | async-done | bytes 655392 | tf_op jit(solution)/shard_map/all_to_all | solution.py:449
  39.5 0.4 key_state.1
  40.0 5.6 %collective-permute-start.1 = (f32[80,224]{1,0:T(8,128)S(1)}, f32[80,224]{1,0:T(8,128)S(1)}, u32[]{:S(2)}, u32[]{:S(2)}) collective-permute-start(f32[80,224]{1,0:T(8,128)S(1)} %get-tuple-element.45), channel_id=1, source_target_pairs={{0,16},{1,17},{2,18},{3,19},{4,20},{5,21},{6,22},{7,23},{8,24},{9,... | collective-permute-start | bytes 215048 | tf_op jit(solution)/shard_map/ppermute | solution.py:455
  45.5 1.1 %inside_chunks.1 = (f32[8,256,256]{2,1,0:T(8,128)S(1)}, f32[8,80,256]{2,1,0:T(8,128)S(1)}, bf16[8,224,256]{2,1,0:T(8,128)(2,1)S(1)}) custom-call(bf16[16,160,128]{2,1,0:T(8,128)(2,1)S(1)} %all-to-all-done.x_ref), custom_call_target="tpu_custom_call" | custom-call | tf_op jit(solution)/shard_map/inside_chunks/pallas_call | solution.py:203
  46.6 1.0 %collective-permute-done.1.half_ref = f32[80,224]{1,0:T(8,128)S(1)} collective-permute-done((f32[80,224]{1,0:T(8,128)S(1)}, f32[80,224]{1,0:T(8,128)S(1)}, u32[]{:S(2)}, u32[]{:S(2)}) %collective-permute-start.1) | collective-permute-done | bytes 71712 | tf_op jit(solution)/shard_map/ppermute | solution.py:455
  47.6 1.1 %linear_output.1 = (bf16[8,64,256]{2,1,0:T(8,128)(2,1)S(1)}, bf16[8,80,256]{2,1,0:T(8,128)(2,1)S(1)}, bf16[8,80,256]{2,1,0:T(8,128)(2,1)S(1)}, f32[8,80,224]{2,1,0:T(8,128)S(1)}, f32[80,224]{1,0:T(8,128)S(1)}) custom-call(bf16[16,160,128]{2,1,0:T(8,128)(2,1)S(1)} %all-to-all-done.x_ref, f32[8,80,224]{2,1,0:T(8,128)S(1)} %get-tuple-element.43.pref_ref, ...), custom_call_target="tpu_custom_call" | custom-call | tf_op jit(solution)/shard_map/linear_output/pallas_call | solution.py:245
  48.7 1.3 %collective-permute-start.3 = (f32[80,224]{1,0:T(8,128)S(1)}, f32[80,224]{1,0:T(8,128)S(1)}, u32[]{:S(2)}, u32[]{:S(2)}) collective-permute-start(f32[80,224]{1,0:T(8,128)S(1)} %get-tuple-element.58), channel_id=1, source_target_pairs={{16,0},{17,1},{18,2},{19,3},{20,4},{21,5},{22,6},{23,7},{24,8},{25... | collective-permute-start | bytes 215048 | tf_op jit(solution)/shard_map/ppermute | solution.py:459
  50.0 2.9 %query_grads.1 = (bf16[8,16,256]{2,1,0:T(8,128)(2,1)S(1)}, f32[8,80,256]{2,1,0:T(8,128)S(1)}) custom-call(bf16[16,160,128]{2,1,0:T(8,128)(2,1)S(1)} %all-to-all-done.x_ref, f32[8,256,256]{2,1,0:T(8,128)S(1)} %get-tuple-element.50.scores_ref, f32[8,80,224]{2,1,0:T(8,128)S(1)} %get-tuple-element.43.pref_ref, f32[80,224]{1,0:T(8,128)S(1)} %collective-permute-done.1.half_ref, ...), custom_call_target="tpu_custom_call" | custom-call | tf_op jit(solution)/shard_map/query_grads/pallas_call | solution.py:279
  52.9 0.0 collective-permute-done.2.halo_ref
  52.9 3.6 %collective-permute-done.3.half_ref = f32[80,224]{1,0:T(8,128)S(1)} collective-permute-done((f32[80,224]{1,0:T(8,128)S(1)}, f32[80,224]{1,0:T(8,128)S(1)}, u32[]{:S(2)}, u32[]{:S(2)}) %collective-permute-start.3) | collective-permute-done | bytes 71712 | tf_op jit(solution)/shard_map/ppermute | solution.py:459
  56.5 0.9 %key_grads.1 = bf16[16,160,128]{2,1,0:T(8,128)(2,1)S(1)} custom-call(bf16[16,160,128]{2,1,0:T(8,128)(2,1)S(1)} %all-to-all-done.x_ref, bf16[8,64,256]{2,1,0:T(8,128)(2,1)S(1)} %get-tuple-element.49.lin_ref, bf16[8,16,256]{2,1,0:T(8,128)(2,1)S(1)} %get-tuple-element.55.dq_ref, f32[8,80,256]{2,1,0:T(8,128)S(1)} %get-tuple-element.56.part_ref, ...), custom_call_target="tpu_custom_call" | custom-call | tf_op jit(solution)/shard_map/key_grads/pallas_call | solution.py:314
  57.4 26.4 %all_to_all.10.y_ref = bf16[16,160,128]{2,1,0:T(8,128)(2,1)S(1)} all-to-all(bf16[16,160,128]{2,1,0:T(8,128)(2,1)S(1)} %key_grads.1), channel_id=1, replica_groups=mesh['dp'=8,'half'=2,'head'=16] {'head'}, dimensions={0} | all-to-all | bytes 1310720 | tf_op jit(solution)/shard_map/all_to_all | solution.py:462
  83.8 1.1 %finish.1 = (bf16[128,1024]{1,0:T(8,128)(2,1)}, bf16[128,256]{1,0:T(8,128)(2,1)}, bf16[128,256]{1,0:T(8,128)(2,1)}, bf16[128,1024]{1,0:T(8,128)(2,1)}, bf16[128,1024]{1,0:T(8,128)(2,1)}) custom-call(bf16[16,160,128]{2,1,0:T(8,128)(2,1)S(1)} %all_to_all.10.y_ref, f32[128,1024]{1,0:T(8,128)S(1)} %get-tuple-element.60.out_ref, ...), custom_call_target="tpu_custom_call" | custom-call | tf_op jit(solution)/shard_map/finish/pallas_call | solution.py:432
Async XLA Ops:
  0.6 20.0 %copy-start.2 = (bf16[128,1024]{1,0:T(8,128)(2,1)S(1)}, bf16[128,1024]{1,0:T(8,128)(2,1)}, u32[]{:S(2)}) copy-start(bf16[128,1024]{1,0:T(8,128)(2,1)} %g_ref.1) | copy-start | bytes 786436
  0.6 20.0 %copy-start.1 = (bf16[128,1024]{1,0:T(8,128)(2,1)S(1)}, bf16[128,1024]{1,0:T(8,128)(2,1)}, u32[]{:S(2)}) copy-start(bf16[128,1024]{1,0:T(8,128)(2,1)} %v_ref.1) | copy-start | bytes 786436
  0.7 20.0 %copy-start = (bf16[128,1024]{1,0:T(8,128)(2,1)S(1)}, bf16[128,1024]{1,0:T(8,128)(2,1)}, u32[]{:S(2)}) copy-start(bf16[128,1024]{1,0:T(8,128)(2,1)} %k_ref.1) | copy-start | bytes 786436
  3.4 16.5 %collective-permute-start = (bf16[2,128,1024]{2,1,0:T(8,128)(2,1)}, bf16[2,128,1024]{2,1,0:T(8,128)(2,1)S(1)}, u32[]{:S(2)}, u32[]{:S(2)}) collective-permute-start(bf16[2,128,1024]{2,1,0:T(8,128)(2,1)} %get-tuple-element.39), channel_id=1, source_target_pairs={{0,1},{1,2},{2,3},{3,4},{4,5},{5,6},{6,7},{7,8},{8,9},{9,10},{10,1... | collective-permute-start | bytes 1572872 | tf_op jit(solution)/shard_map/ppermute | solution.py:448
  7.3 32.3 %all-to-all-start = ((bf16[16,160,128]{2,1,0:T(8,128)(2,1)}), bf16[16,160,128]{2,1,0:T(8,128)(2,1)S(1)}, u32[]{:S(2)}, u32[]{:S(2)}) async-start(bf16[16,160,128]{2,1,0:T(8,128)(2,1)} %get-tuple-element.38), calls=%async_computation | async-start | bytes 1310720 | tf_op jit(solution)/shard_map/all_to_all | solution.py:449
  19.9 0.8 copy-start.3
  20.7 1.0 %copy-start.4 = (bf16[2,128,1024]{2,1,0:T(8,128)(2,1)S(1)}, bf16[2,128,1024]{2,1,0:T(8,128)(2,1)}, u32[]{:S(2)}) copy-start(bf16[2,128,1024]{2,1,0:T(8,128)(2,1)} %copy-done.3) | copy-start | bytes 1572868
  21.7 0.9 %copy-start.5 = (bf16[128,1024]{1,0:T(8,128)(2,1)S(1)}, bf16[128,1024]{1,0:T(8,128)(2,1)}, u32[]{:S(2)}) copy-start(bf16[128,1024]{1,0:T(8,128)(2,1)} %q_ref.1) | copy-start | bytes 786436
  30.8 22.1 %collective-permute-start.2 = (bf16[2,128,1024]{2,1,0:T(8,128)(2,1)S(1)}, bf16[2,128,1024]{2,1,0:T(8,128)(2,1)S(1)}, u32[]{:S(2)}, u32[]{:S(2)}) collective-permute-start(bf16[2,128,1024]{2,1,0:T(8,128)(2,1)S(1)} %get-tuple-element.54), channel_id=1, source_target_pairs={{1,0},{2,1},{3,2},{4,3},{5,4},{6,5},{7,6},{8,7},{9,8},{10,9},{11,1... | collective-permute-start | bytes 1572872 | tf_op jit(solution)/shard_map/ppermute | solution.py:452
  40.0 7.6 %collective-permute-start.1 = (f32[80,224]{1,0:T(8,128)S(1)}, f32[80,224]{1,0:T(8,128)S(1)}, u32[]{:S(2)}, u32[]{:S(2)}) collective-permute-start(f32[80,224]{1,0:T(8,128)S(1)} %get-tuple-element.45), channel_id=1, source_target_pairs={{0,16},{1,17},{2,18},{3,19},{4,20},{5,21},{6,22},{7,23},{8,24},{9,... | collective-permute-start | bytes 215048 | tf_op jit(solution)/shard_map/ppermute | solution.py:455
  48.7 7.8 %collective-permute-start.3 = (f32[80,224]{1,0:T(8,128)S(1)}, f32[80,224]{1,0:T(8,128)S(1)}, u32[]{:S(2)}, u32[]{:S(2)}) collective-permute-start(f32[80,224]{1,0:T(8,128)S(1)} %get-tuple-element.58), channel_id=1, source_target_pairs={{16,0},{17,1},{18,2},{19,3},{20,4},{21,5},{22,6},{23,7},{24,8},{25... | collective-permute-start | bytes 215048 | tf_op jit(solution)/shard_map/ppermute | solution.py:459

commit v2 on v1

--- a/solution.py
+++ b/solution.py
@@ -34,7 +34,7 @@
 
 
 def flip(x):
-    return jnp.transpose(x.astype(F32)).astype(BF)
+    return jnp.transpose(x)
 
 
 def pack_kernel(
@@ -256,23 +256,29 @@
     )(x, pref, half, numer, feat)
 
 
-def query_kernel(x_ref, scores_ref, pref_ref, half_ref, dhi_ref, dlo_ref, dq_ref, part_ref):
+def query_kernel(
+    x_ref, scores_ref, pref_ref, half_ref, dhi_ref, dlo_ref, dq_ref, part_ref,
+    feat_ref, low_ref,
+):
     causal = causal_mask()
     for c in range(STEPS):
-        key = rows_of(x_ref, c, 0, 16)
-        query = rows_of(x_ref, c, 80, 96)
+        d_hi, d_lo = dhi_ref[c], dlo_ref[c]
         ones_t = flip(with_ones(rows_of(x_ref, c, 16, 80)))
+        d_kernel = nn(ones_t, d_hi) + nn(ones_t, d_lo)
+        low_ref[c] = jnp.where(causal, d_kernel * (1.0 + scores_ref[c]), 0.0).astype(BF)
+    for c in range(STEPS):
         d_hi, d_lo = dhi_ref[c], dlo_ref[c]
+        turned_hi, turned_lo = split(jnp.transpose(pref_ref[c] + half_ref[...]))
+        feat_ref[c] = nn(turned_hi, d_hi) + nn(turned_lo, d_hi) + nn(turned_hi, d_lo)
+    for c in range(STEPS):
         scores = scores_ref[c]
         kernel = jnp.where(causal, 1.0 + scores + 0.5 * scores * scores, 0.0).astype(BF)
-        turned_hi, turned_lo = split(jnp.transpose(pref_ref[c] + half_ref[...]))
-        d_feat = nn(turned_hi, d_hi) + nn(turned_lo, d_hi) + nn(turned_hi, d_lo)
-        d_kernel = nn(ones_t, d_hi) + nn(ones_t, d_lo)
-        d_scores = jnp.where(causal, d_kernel * (1.0 + scores), 0.0).astype(BF)
-        d_query = pull(query.astype(F32), d_feat, False) + nn(key, d_scores) * 0.25
-        dq_ref[c] = d_query.astype(BF)
-        part_ref[c, 0:64] = nt(d_hi[0:64], kernel)
-        part_ref[c, 64:80] = nt(query, d_scores) * 0.25
+        part_ref[c, 0:64] = nt(dhi_ref[c, 0:64], kernel)
+        part_ref[c, 64:80] = nt(rows_of(x_ref, c, 80, 96), low_ref[c]) * 0.25
+    for c in range(STEPS):
+        query = rows_of(x_ref, c, 80, 96).astype(F32)
+        own = nn(rows_of(x_ref, c, 0, 16), low_ref[c]) * 0.25
+        dq_ref[c] = (pull(query, feat_ref[c], False) + own).astype(BF)
 
 
 def query_grads(x, scores, pref, half, d_hi, d_lo):
@@ -282,6 +288,10 @@
             jax.ShapeDtypeStruct((STEPS, FD, WIDE), BF),
             jax.ShapeDtypeStruct((STEPS, ROWS, WIDE), F32),
         ),
+        scratch_shapes=[
+            pltpu.VMEM((STEPS, FEAT, WIDE), F32),
+            pltpu.VMEM((STEPS, WIDE, WIDE), BF),
+        ],
         compiler_params=PARAMS,
         name="query_grads",
     )(x, scores, pref, half, d_hi, d_lo)
@@ -320,9 +330,15 @@
 
 
 def window_kernel(
-    first_ref, q_ref, k_ref, v_ref, g_ref, halo_ref,
-    out_ref, dq_ref, dk_ref, dv_ref, back_hbm, back_ref, sems,
+    first_ref, q_hbm, k_hbm, v_hbm, g_hbm, halo_ref,
+    out_ref, dq_ref, dk_ref, dv_ref, back_ref,
+    q_ref, k_ref, v_ref, g_ref, logit_ref, d_attn_ref, low_ref, d_low_ref, sems,
 ):
+    copies = []
+    pairs_in = ((k_hbm, k_ref), (q_hbm, q_ref), (v_hbm, v_ref), (g_hbm, g_ref))
+    for i, (source, target) in enumerate(pairs_in):
+        copies.append(pltpu.make_async_copy(source, target, sems.at[i]))
+        copies[i].start()
     source = lax.broadcasted_iota(jnp.int32, (TOK, 2 * TOK), 0)
     target = lax.broadcasted_iota(jnp.int32, (TOK, 2 * TOK), 1) % TOK
     own = source <= target
@@ -336,61 +352,91 @@
     lane_b = (col >= DH).astype(F32).astype(BF)
     blocked = jnp.where(first_ref[0] == 1, -1e30, 0.0)
 
-    def both(x):
-        return jnp.concatenate([x * lane_a, x * lane_b], 0)
-
-    copies = []
-    for p in range(H // 2):
-        cols = slice(p * 128, (p + 1) * 128)
-        key, key_p = k_ref[:, cols], halo_ref[0, :, cols]
-        value, value_p = v_ref[:, cols], halo_ref[1, :, cols]
-        query2 = both(q_ref[:, cols])
-        grad2 = both(g_ref[:, cols])
-        logits = jnp.where(own, nt(key, query2) * 0.125, nt(key_p, query2) * 0.125 + blocked)
+    lane_a8 = lane_a * 0.125
+    lane_b8 = lane_b * 0.125
+    wide_a = jnp.concatenate([lane_a, lane_a], 0)
+    wide_b = jnp.concatenate([lane_b, lane_b], 0)
+    wide_a8 = jnp.concatenate([lane_a8, lane_a8], 0)
+    wide_b8 = jnp.concatenate([lane_b8, lane_b8], 0)
+
+    pairs = range(H // 2)
+
+    def cols_of(p):
+        return slice(p * 128, (p + 1) * 128)
+
+    def query_rows(p):
+        query = q_ref[:, cols_of(p)]
+        return jnp.concatenate([query * lane_a8, query * lane_b8], 0)
+
+    def grad_rows(p):
+        grad = g_ref[:, cols_of(p)]
+        return jnp.concatenate([grad * lane_a, grad * lane_b], 0)
+
+    def key_rows(p):
+        return jnp.concatenate([k_ref[:, cols_of(p)], halo_ref[0, :, cols_of(p)]], 0)
+
+    def value_rows(p):
+        return jnp.concatenate([v_ref[:, cols_of(p)], halo_ref[1, :, cols_of(p)]], 0)
+
+    copies[0].wait()
+    copies[1].wait()
+    for p in pairs:
+        scores = nt(key_rows(p), query_rows(p))
+        logit_ref[p] = jnp.where(own, scores[0:TOK], scores[TOK:] + blocked)
+    copies[2].wait()
+    copies[3].wait()
+    for p in pairs:
+        d_both = nt(value_rows(p), grad_rows(p))
+        d_attn_ref[p] = jnp.where(own, d_both[0:TOK], d_both[TOK:])
+    for p in pairs:
+        logits = logit_ref[p]
         shifted = jnp.exp(logits - jnp.max(logits, 0, keepdims=True))
         attn = shifted * (1.0 / jnp.sum(shifted, 0, keepdims=True))
-        attn_low = attn.astype(BF)
+        logit_ref[p] = attn
+        low_ref[p] = attn.astype(BF)
+    for p in pairs:
         pieces = []
         for i in range(2):
-            turned = flip(attn_low[:, i * TOK : (i + 1) * TOK])
+            turned = flip(low_ref[p, :, i * TOK : (i + 1) * TOK])
             pieces += [turned * own_t, turned * prev_t]
-        values4 = jnp.concatenate(
-            [value * lane_a, value_p * lane_a, value * lane_b, value_p * lane_b], 0
+        values = value_rows(p)
+        result = nn(
+            jnp.concatenate(pieces, 1), jnp.concatenate([values * wide_a, values * wide_b], 0)
         )
-        result = nn(jnp.concatenate(pieces, 1), values4)
-        out_ref[:, cols] = result
-        inner_t = jnp.transpose(result * g_ref[:, cols].astype(F32))
+        out_ref[:, cols_of(p)] = result
+    for p in pairs:
+        inner_t = jnp.transpose(out_ref[:, cols_of(p)] * g_ref[:, cols_of(p)].astype(F32))
         inner = jnp.concatenate(
             [jnp.sum(inner_t[0:64], 0, keepdims=True), jnp.sum(inner_t[64:128], 0, keepdims=True)],
             1,
         )
-        d_attn = jnp.where(own, nt(value, grad2), nt(value_p, grad2))
-        d_logits = (attn * (d_attn - inner)).astype(BF)
+        d_low_ref[p] = (logit_ref[p] * (d_attn_ref[p] - inner)).astype(BF)
+    for p in pairs:
+        cols = cols_of(p)
+        d_logits, attn_low = d_low_ref[p], low_ref[p]
         pieces = []
         for i in range(2):
             turned = flip(d_logits[:, i * TOK : (i + 1) * TOK])
             pieces += [turned * own_t, turned * prev_t]
-        keys4 = jnp.concatenate([key * lane_a, key_p * lane_a, key * lane_b, key_p * lane_b], 0)
-        dq_ref[:, cols] = (nn(jnp.concatenate(pieces, 1), keys4) * 0.125).astype(BF)
-        dk_ref[:, cols] = nn(d_logits * own_low, query2) * 0.125
-        back_ref[0, :, cols] = (nn(d_logits * prev_low, query2) * 0.125).astype(BF)
-        dv_ref[:, cols] = nn(attn_low * own_low, grad2)
-        back_ref[1, :, cols] = nn(attn_low * prev_low, grad2).astype(BF)
-        copies.append(
-            pltpu.make_async_copy(back_ref.at[:, :, cols], back_hbm.at[:, :, cols], sems.at[p])
-        )
-        copies[-1].start()
-    for copy in copies:
-        copy.wait()
+        keys = key_rows(p)
+        dq_ref[:, cols] = nn(
+            jnp.concatenate(pieces, 1), jnp.concatenate([keys * wide_a8, keys * wide_b8], 0)
+        ).astype(BF)
+        d_keys = nn(jnp.concatenate([d_logits * own_low, d_logits * prev_low], 0), query_rows(p))
+        dk_ref[:, cols] = d_keys[0:TOK]
+        back_ref[0, :, cols] = d_keys[TOK:].astype(BF)
+        d_values = nn(jnp.concatenate([attn_low * own_low, attn_low * prev_low], 0), grad_rows(p))
+        dv_ref[:, cols] = d_values[0:TOK]
+        back_ref[1, :, cols] = d_values[TOK:].astype(BF)
 
 
 def window(first, q, k, v, g, halo):
     wide = (TOK, H * DH)
-    vmem = pl.BlockSpec(memory_space=pltpu.VMEM)
+    hbm = pl.BlockSpec(memory_space=pltpu.HBM)
     return pl.pallas_call(
         window_kernel,
-        in_specs=[pl.BlockSpec(memory_space=pltpu.SMEM)] + [vmem] * 5,
-        out_specs=(vmem,) * 4 + (pl.BlockSpec(memory_space=pltpu.HBM),),
+        in_specs=[pl.BlockSpec(memory_space=pltpu.SMEM)] + [hbm] * 4 + [pl.BlockSpec()],
+        out_specs=(pl.BlockSpec(),) * 5,
         out_shape=(
             jax.ShapeDtypeStruct(wide, F32),
             jax.ShapeDtypeStruct(wide, BF),
@@ -398,26 +444,51 @@
             jax.ShapeDtypeStruct(wide, F32),
             jax.ShapeDtypeStruct((2,) + wide, BF),
         ),
-        scratch_shapes=[pltpu.VMEM((2,) + wide, BF), pltpu.SemaphoreType.DMA((8,))],
+        scratch_shapes=[
+            pltpu.VMEM(wide, BF),
+            pltpu.VMEM(wide, BF),
+            pltpu.VMEM(wide, BF),
+            pltpu.VMEM(wide, BF),
+            pltpu.VMEM((8, TOK, 2 * TOK), F32),
+            pltpu.VMEM((8, TOK, 2 * TOK), F32),
+            pltpu.VMEM((8, TOK, 2 * TOK), BF),
+            pltpu.VMEM((8, TOK, 2 * TOK), BF),
+            pltpu.SemaphoreType.DMA((4,)),
+        ],
         compiler_params=PARAMS,
         cost_estimate=pl.CostEstimate(
-            flops=50_000_000_000, transcendentals=0, bytes_accessed=6_000_000
+            flops=5_000_000_000, transcendentals=0, bytes_accessed=6_000_000
         ),
         name="window",
-    )(first, q, k, v, g, halo)
-
-
-def finish_kernel(
-    y_ref, out_ref, dk_ref, dv_ref, halo_ref, mixed_ref, gq_ref, gk_ref, gkw_ref, gv_ref
-):
+    )(first, *(pltpu.with_memory_space_constraint(a, pltpu.HBM) for a in (q, k, v, g)), halo)
+
+
+def settle_kernel(dk_ref, dv_ref, halo_ref, gkw_ref, sum_ref):
+    gkw_ref[...] = (dk_ref[...] + halo_ref[0].astype(F32)).astype(BF)
+    sum_ref[...] = dv_ref[...] + halo_ref[1].astype(F32)
+
+
+def settle(dk, dv, halo):
+    wide = (TOK, H * DH)
+    return pl.pallas_call(
+        settle_kernel,
+        out_shape=(jax.ShapeDtypeStruct(wide, BF), jax.ShapeDtypeStruct(wide, F32)),
+        compiler_params=PARAMS,
+        cost_estimate=pl.CostEstimate(
+            flops=50_000_000_000, transcendentals=0, bytes_accessed=2_000_000
+        ),
+        name="settle",
+    )(dk, dv, halo)
+
+
+def finish_kernel(y_ref, out_ref, dv_ref, mixed_ref, gq_ref, gk_ref, gv_ref):
     for p in range(8):
         cols = slice(p * 128, (p + 1) * 128)
-        pair = jnp.concatenate([y_ref[2 * p, 0:64], y_ref[2 * p + 1, 0:64]], 0)
-        mixed_ref[:, cols] = (jnp.transpose(pair.astype(F32)) + out_ref[:, cols]).astype(BF)
-        pair = jnp.concatenate([y_ref[2 * p, 80:144], y_ref[2 * p + 1, 80:144]], 0)
-        own = dv_ref[:, cols] + halo_ref[1, :, cols].astype(F32)
-        gv_ref[:, cols] = (jnp.transpose(pair.astype(F32)) + own).astype(BF)
-        gkw_ref[:, cols] = (dk_ref[:, cols] + halo_ref[0, :, cols].astype(F32)).astype(BF)
+        for ref, add_ref, row in ((mixed_ref, out_ref, 0), (gv_ref, dv_ref, 80)):
+            pair = jnp.concatenate(
+                [y_ref[2 * p, row : row + 64], y_ref[2 * p + 1, row : row + 64]], 0
+            )
+            ref[:, cols] = (flip(pair).astype(F32) + add_ref[:, cols]).astype(BF)
     for j in range(2):
         cols = slice(j * 128, (j + 1) * 128)
         for ref, row in ((gq_ref, 64), (gk_ref, 144)):
@@ -426,15 +497,15 @@
             )
 
 
-def finish(y, out, dk, dv, halo):
+def finish(y, out, dv):
     wide = jax.ShapeDtypeStruct((TOK, H * DH), BF)
     thin = jax.ShapeDtypeStruct((TOK, H * FD), BF)
     return pl.pallas_call(
         finish_kernel,
-        out_shape=(wide, thin, thin, wide, wide),
+        out_shape=(wide, thin, thin, wide),
         compiler_params=PARAMS,
         name="finish",
-    )(y, out, dk, dv, halo)
+    )(y, out, dv)
 
 
 def local(q_lin, k_lin, q_win, k_win, values, grad_out):
@@ -448,19 +519,21 @@
     halo = lax.ppermute(halo, seq, later)
     x = spread(own)
     first = (lax.axis_index(seq) == 0).astype(jnp.int32).reshape(1)
-    out, dq_win, dk, dv, back_halo = window(first, q_win, k_win, values, grad_out, halo)
-    back_halo = lax.ppermute(back_halo, seq, earlier)
-    x, dk, dv = lax.optimization_barrier((x, dk, dv))
     pref, total, key_feat = key_state(x)
     half = lax.ppermute(total, "half", [(0, 1)])
     scores, numer, query_feat = inside(x)
     numer, half = lax.optimization_barrier((numer, half))
     lin, d_hi, d_lo, state, total = output(x, pref, half, numer, query_feat)
     next_half = lax.ppermute(total, "half", [(1, 0)])
+    d_hi, halo = lax.optimization_barrier((d_hi, halo))
+    out, dq_win, dk, dv, back_halo = window(first, q_win, k_win, values, grad_out, halo)
+    d_hi, back_halo, next_half = lax.optimization_barrier((d_hi, back_halo, next_half))
+    back_halo = lax.ppermute(back_halo, seq, earlier)
     dq, part = query_grads(x, scores, pref, half, d_hi, d_lo)
-    dq, back_halo = lax.optimization_barrier((dq, back_halo))
     y = spread(key_grads(x, lin, dq, part, state, next_half, key_feat))
-    mixed, gq, gk, gkw, gv = finish(y, out, dk, dv, back_halo)
+    gkw, dv = settle(dk, dv, back_halo)
+    y, gkw, dv = lax.optimization_barrier((y, gkw, dv))
+    mixed, gq, gk, gv = finish(y, out, dv)
     return (mixed, gq, gk, dq_win, gkw, gv)
 
 

time: 85.3 us -> 82.2 us (0.964)
  blocking collectives: 26.4 us -> 0 us
  waiting for transfers between devices: 15.9 us -> 38 us
  starting transfers between devices: 20.7 us -> 25.6 us
  Pallas kernels: 18.4 us -> 15.2 us
    all_to_all x1 -> x0, blocking collectives: 26.4 us -> none  [local(): y = spread(key_grads(x, lin, dq, part, state, next_half, key_feat))]
    ppermute x1, waiting for transfers between devices: 0.01 us -> 13.1 us  [local(): back_halo = lax.ppermute(back_halo, seq, earlier)]
    all_to_all x1, waiting for transfers between devices: 7.41 us -> 15.7 us  [local(): x = spread(own)]
    all_to_all x0 -> x1, starting transfers between devices: none -> 4.81 us  [local(): y = spread(key_grads(x, lin, dq, part, state, next_half, key_feat))]
    ppermute x1, waiting for transfers between devices: 3.91 us -> 0.01 us  [local(): halo = lax.ppermute(halo, seq, later)]
    pallas_call x1, Pallas kernels: 8.14 us -> 4.29 us  [window(): pl.pallas_call(window_kernel, in_specs=[pl.BlockSpec(memory_space=pltpu.S...]
    all_to_all x0 -> x1, waiting for transfers between devices: none -> 3.3 us  [local(): y = spread(key_grads(x, lin, dq, part, state, next_half, key_feat))]
    ppermute x1, waiting for transfers between devices: 0.96 us -> 3.62 us  [local(): half = lax.ppermute(total, 'half', [(0, 1)])]
  transfers between devices with their start and end apart: 5 -> 6, of which waited for: 4 -> 5; matrix products, arithmetic and copies ran while one was open for 0% -> 0% of each run, Pallas kernels for 16% -> 14%
where the time goes in v2:
time: 82.2 us; the launch traced here: 81.7 us
  waiting for transfers between devices  38 us (46%)
  starting transfers between devices  25.6 us (31%)
  Pallas kernels  15.2 us (18%)
  local copies, waits for them, and re-layouts  2.09 us (3%)
    all_to_all x1, waiting for transfers between devices, local(): x = spread(own)  15.7 us
    ppermute x1, waiting for transfers between devices, local(): back_halo = lax.ppermute(back_halo, seq, earlier)  13.1 us
    all_to_all x1, starting transfers between devices, local(): x = spread(own)  9.59 us
    all_to_all x1, starting transfers between devices, local(): y = spread(key_grads(x, lin, dq, part, state, next_half, key_feat))  4.81 us
    ppermute x1, starting transfers between devices, local(): half = lax.ppermute(total, 'half', [(0, 1)])  4.8 us
    pallas_call x1, Pallas kernels, window(): pl.pallas_call(window_kernel, in_specs=[pl.BlockSpec(memory_space=pltpu.S...  4.29 us
    ppermute x1, starting transfers between devices, local(): halo = lax.ppermute(halo, seq, later)  3.85 us
    ppermute x1, waiting for transfers between devices, local(): half = lax.ppermute(total, 'half', [(0, 1)])  3.62 us
  transfers between devices with their start and end apart: 6, of which 5 were waited for; matrix products, arithmetic and copies ran while one was open for 0% of the time, Pallas kernels for 14%

profile of v2, /device:TPU:6, one launch (start us, length us, event | category | flops | bytes accessed | tf_op | source)
XLA Modules:
  0.0 81.7 jit_solution(11884840116708870942)
XLA Ops:
  0.6 2.7 %pack.1 = (bf16[16,160,128]{2,1,0:T(8,128)(2,1)}, bf16[2,128,1024]{2,1,0:T(8,128)(2,1)}) custom-call(bf16[128,256]{1,0:T(8,128)(2,1)} %ql_hbm.1, bf16[128,256]{1,0:T(8,128)(2,1)} %kl_hbm.1, bf16[128,1024]{1,0:T(8,128)(2,1)} %k_hbm.1, bf16[128,1024]{1,0:T(8,128)(2,1)} %v_hbm.3, bf16[128,1024]{1,0:T(8,128)(2,1)} %g_hbm.3), custom_call_target="tpu_custom_call" | custom-call | tf_op jit(solution)/shard_map/pack/pallas_call | solution.py:84
  3.3 9.6 %all-to-all-start = ((bf16[16,160,128]{2,1,0:T(8,128)(2,1)}), bf16[16,160,128]{2,1,0:T(8,128)(2,1)S(1)}, u32[]{:S(2)}, u32[]{:S(2)}) async-start(bf16[16,160,128]{2,1,0:T(8,128)(2,1)} %get-tuple-element.42), calls=%async_computation | async-start | bytes 1310720 | tf_op jit(solution)/shard_map/all_to_all | solution.py:520
  12.9 3.9 %collective-permute-start.1 = (bf16[2,128,1024]{2,1,0:T(8,128)(2,1)}, bf16[2,128,1024]{2,1,0:T(8,128)(2,1)S(1)}, u32[]{:S(2)}, u32[]{:S(2)}) collective-permute-start(bf16[2,128,1024]{2,1,0:T(8,128)(2,1)} %get-tuple-element.52), channel_id=1, source_target_pairs={{0,1},{1,2},{2,3},{3,4},{4,5},{5,6},{6,7},{7,8},{8,9},{9,10},{10,1... | collective-permute-start | bytes 1572872 | tf_op jit(solution)/shard_map/ppermute | solution.py:519
  16.8 15.7 %all-to-all-done.x_ref = bf16[16,160,128]{2,1,0:T(8,128)(2,1)S(1)} async-done(((bf16[16,160,128]{2,1,0:T(8,128)(2,1)}), bf16[16,160,128]{2,1,0:T(8,128)(2,1)S(1)}, u32[]{:S(2)}, u32[]{:S(2)}) %all-to-all-start) | async-done | bytes 655392 | tf_op jit(solution)/shard_map/all_to_all | solution.py:520
  32.5 0.4 key_state.1
  32.9 4.8 %collective-permute-start = (f32[80,224]{1,0:T(8,128)S(1)}, f32[80,224]{1,0:T(8,128)S(1)}, u32[]{:S(2)}, u32[]{:S(2)}) collective-permute-start(f32[80,224]{1,0:T(8,128)S(1)} %get-tuple-element.45), channel_id=1, source_target_pairs={{0,16},{1,17},{2,18},{3,19},{4,20},{5,21},{6,22},{7,23},{8,24},{9,... | collective-permute-start | bytes 215048 | tf_op jit(solution)/shard_map/ppermute | solution.py:523
  37.7 1.0 %inside_chunks.1 = (f32[8,256,256]{2,1,0:T(8,128)S(1)}, f32[8,80,256]{2,1,0:T(8,128)S(1)}, bf16[8,224,256]{2,1,0:T(8,128)(2,1)S(1)}) custom-call(bf16[16,160,128]{2,1,0:T(8,128)(2,1)S(1)} %all-to-all-done.x_ref), custom_call_target="tpu_custom_call" | custom-call | tf_op jit(solution)/shard_map/inside_chunks/pallas_call | solution.py:203
  38.8 3.6 %collective-permute-done.half_ref = f32[80,224]{1,0:T(8,128)S(1)} collective-permute-done((f32[80,224]{1,0:T(8,128)S(1)}, f32[80,224]{1,0:T(8,128)S(1)}, u32[]{:S(2)}, u32[]{:S(2)}) %collective-permute-start) | collective-permute-done | bytes 71712 | tf_op jit(solution)/shard_map/ppermute | solution.py:523
  42.4 1.1 %linear_output.1 = (bf16[8,64,256]{2,1,0:T(8,128)(2,1)S(1)}, bf16[8,80,256]{2,1,0:T(8,128)(2,1)S(1)}, bf16[8,80,256]{2,1,0:T(8,128)(2,1)S(1)}, f32[8,80,224]{2,1,0:T(8,128)S(1)}, f32[80,224]{1,0:T(8,128)S(1)}) custom-call(bf16[16,160,128]{2,1,0:T(8,128)(2,1)S(1)} %all-to-all-done.x_ref, f32[8,80,224]{2,1,0:T(8,128)S(1)} %get-tuple-element.43.pref_ref, ...), custom_call_target="tpu_custom_call" | custom-call | tf_op jit(solution)/shard_map/linear_output/pallas_call | solution.py:245
  43.5 0.0 collective-permute-done.1.halo_ref
  43.5 1.3 %collective-permute-start.2 = (f32[80,224]{1,0:T(8,128)S(1)}, f32[80,224]{1,0:T(8,128)S(1)}, u32[]{:S(2)}, u32[]{:S(2)}) collective-permute-start(f32[80,224]{1,0:T(8,128)S(1)} %get-tuple-element.56), channel_id=1, source_target_pairs={{16,0},{17,1},{18,2},{19,3},{20,4},{21,5},{22,6},{23,7},{24,8},{25... | collective-permute-start | bytes 215048 | tf_op jit(solution)/shard_map/ppermute | solution.py:527
  44.8 4.3 %window.1 = (f32[128,1024]{1,0:T(8,128)S(1)}, bf16[128,1024]{1,0:T(8,128)(2,1)}, f32[128,1024]{1,0:T(8,128)S(1)}, f32[128,1024]{1,0:T(8,128)S(1)}, bf16[2,128,1024]{2,1,0:T(8,128)(2,1)}) custom-call(s32[1]{0:T(128)} %bitcast.first_ref, bf16[128,1024]{1,0:T(8,128)(2,1)} %q_hbm.1, bf16[128,1024]{1,0:T(8,128)(2,1)} %k_hbm.1, bf16[128,1024]{1,0:T(8,128)(2,1)} %v_hbm.3, ...), custom_call_target="tpu_custom_call" | custom-call | flops 5000000000 | bytes 6000000 | tf_op jit(solution)/shard_map/window/pallas_call | solution.py:436
  49.1 0.0 copy-start
  49.1 0.0 copy-start.2
  49.1 2.3 %collective-permute-done.2.half_ref = f32[80,224]{1,0:T(8,128)S(1)} collective-permute-done((f32[80,224]{1,0:T(8,128)S(1)}, f32[80,224]{1,0:T(8,128)S(1)}, u32[]{:S(2)}, u32[]{:S(2)}) %collective-permute-start.2) | collective-permute-done | bytes 71712 | tf_op jit(solution)/shard_map/ppermute | solution.py:527
  51.4 1.3 %collective-permute-start.3 = (bf16[2,128,1024]{2,1,0:T(8,128)(2,1)}, bf16[2,128,1024]{2,1,0:T(8,128)(2,1)S(1)}, u32[]{:S(2)}, u32[]{:S(2)}) collective-permute-start(bf16[2,128,1024]{2,1,0:T(8,128)(2,1)} %get-tuple-element.66), channel_id=1, source_target_pairs={{1,0},{2,1},{3,2},{4,3},{5,4},{6,5},{7,6},{8,7},{9,8},{10,9},{11,1... | collective-permute-start | bytes 1572872 | tf_op jit(solution)/shard_map/ppermute | solution.py:531
  52.7 2.1 %query_grads.1 = (bf16[8,16,256]{2,1,0:T(8,128)(2,1)S(1)}, f32[8,80,256]{2,1,0:T(8,128)S(1)}) custom-call(bf16[16,160,128]{2,1,0:T(8,128)(2,1)S(1)} %all-to-all-done.x_ref, f32[8,256,256]{2,1,0:T(8,128)S(1)} %get-tuple-element.50.scores_ref, f32[8,80,224]{2,1,0:T(8,128)S(1)} %get-tuple-element.43.pref_ref, f32[80,224]{1,0:T(8,128)S(1)} %collective-permute-done.half_ref, ...), custom_call_target="tpu_custom_call" | custom-call | tf_op jit(solution)/shard_map/query_grads/pallas_call | solution.py:285
  54.8 0.0 copy-done
  54.8 0.0 copy-done.2
  54.8 1.7 %key_grads.1 = bf16[16,160,128]{2,1,0:T(8,128)(2,1)} custom-call(bf16[16,160,128]{2,1,0:T(8,128)(2,1)S(1)} %all-to-all-done.x_ref, bf16[8,64,256]{2,1,0:T(8,128)(2,1)S(1)} %get-tuple-element.49.lin_ref, bf16[8,16,256]{2,1,0:T(8,128)(2,1)S(1)} %get-tuple-element.59.dq_ref, f32[8,80,256]{2,1,0:T(8,128)S(1)} %get-tuple-element.60.part_ref, ...), custom_call_target="tpu_custom_call" | custom-call | tf_op jit(solution)/shard_map/key_grads/pallas_call | solution.py:324
  56.5 4.8 %all-to-all-start.1 = ((bf16[16,160,128]{2,1,0:T(8,128)(2,1)}), bf16[16,160,128]{2,1,0:T(8,128)(2,1)S(1)}, u32[]{:S(2)}, u32[]{:S(2)}) async-start(bf16[16,160,128]{2,1,0:T(8,128)(2,1)} %key_grads.1), calls=%async_computation.1 | async-start | bytes 1310720 | tf_op jit(solution)/shard_map/all_to_all | solution.py:533
  61.4 13.1 %collective-permute-done.3.halo_ref = bf16[2,128,1024]{2,1,0:T(8,128)(2,1)S(1)} collective-permute-done((bf16[2,128,1024]{2,1,0:T(8,128)(2,1)}, bf16[2,128,1024]{2,1,0:T(8,128)(2,1)S(1)}, u32[]{:S(2)}, u32[]{:S(2)}) %collective-permute-start.3) | collective-permute-done | bytes 524320 | tf_op jit(solution)/shard_map/ppermute | solution.py:531
  74.5 0.0 copy-start.1
  74.5 1.0 %copy-done.1 = f32[128,1024]{1,0:T(8,128)S(1)} copy-done((f32[128,1024]{1,0:T(8,128)S(1)}, f32[128,1024]{1,0:T(8,128)}, u32[]{:S(2)}) %copy-start.1) | copy-done | bytes 524312
  75.5 0.0 copy-start.3
  75.5 1.0 %copy-done.3 = f32[128,1024]{1,0:T(8,128)S(1)} copy-done((f32[128,1024]{1,0:T(8,128)S(1)}, f32[128,1024]{1,0:T(8,128)}, u32[]{:S(2)}) %copy-start.3) | copy-done | bytes 524312
  76.6 0.8 settle.1
  77.3 3.3 %all-to-all-done.1.y_ref = bf16[16,160,128]{2,1,0:T(8,128)(2,1)S(1)} async-done(((bf16[16,160,128]{2,1,0:T(8,128)(2,1)}), bf16[16,160,128]{2,1,0:T(8,128)(2,1)S(1)}, u32[]{:S(2)}, u32[]{:S(2)}) %all-to-all-start.1) | async-done | bytes 655392 | tf_op jit(solution)/shard_map/all_to_all | solution.py:533
  80.6 1.0 %finish.1 = (bf16[128,1024]{1,0:T(8,128)(2,1)}, bf16[128,256]{1,0:T(8,128)(2,1)}, bf16[128,256]{1,0:T(8,128)(2,1)}, bf16[128,1024]{1,0:T(8,128)(2,1)}) custom-call(bf16[16,160,128]{2,1,0:T(8,128)(2,1)S(1)} %all-to-all-done.1.y_ref, f32[128,1024]{1,0:T(8,128)S(1)} %get-tuple-element.70.out_ref, f32[128,1024]{1,0:T(8,128)S(1)} %get-tuple-element.71.dv_ref), custom_call_target="tpu_custom_call" | custom-call | tf_op jit(solution)/shard_map/finish/pallas_call | solution.py:503
Async XLA Ops:
  3.3 29.2 %all-to-all-start = ((bf16[16,160,128]{2,1,0:T(8,128)(2,1)}), bf16[16,160,128]{2,1,0:T(8,128)(2,1)S(1)}, u32[]{:S(2)}, u32[]{:S(2)}) async-start(bf16[16,160,128]{2,1,0:T(8,128)(2,1)} %get-tuple-element.42), calls=%async_computation | async-start | bytes 1310720 | tf_op jit(solution)/shard_map/all_to_all | solution.py:520
  12.9 30.6 %collective-permute-start.1 = (bf16[2,128,1024]{2,1,0:T(8,128)(2,1)}, bf16[2,128,1024]{2,1,0:T(8,128)(2,1)S(1)}, u32[]{:S(2)}, u32[]{:S(2)}) collective-permute-start(bf16[2,128,1024]{2,1,0:T(8,128)(2,1)} %get-tuple-element.52), channel_id=1, source_target_pairs={{0,1},{1,2},{2,3},{3,4},{4,5},{5,6},{6,7},{7,8},{8,9},{9,10},{10,1... | collective-permute-start | bytes 1572872 | tf_op jit(solution)/shard_map/ppermute | solution.py:519
  32.9 9.5 %collective-permute-start = (f32[80,224]{1,0:T(8,128)S(1)}, f32[80,224]{1,0:T(8,128)S(1)}, u32[]{:S(2)}, u32[]{:S(2)}) collective-permute-start(f32[80,224]{1,0:T(8,128)S(1)} %get-tuple-element.45), channel_id=1, source_target_pairs={{0,16},{1,17},{2,18},{3,19},{4,20},{5,21},{6,22},{7,23},{8,24},{9,... | collective-permute-start | bytes 215048 | tf_op jit(solution)/shard_map/ppermute | solution.py:523
  43.5 7.9 %collective-permute-start.2 = (f32[80,224]{1,0:T(8,128)S(1)}, f32[80,224]{1,0:T(8,128)S(1)}, u32[]{:S(2)}, u32[]{:S(2)}) collective-permute-start(f32[80,224]{1,0:T(8,128)S(1)} %get-tuple-element.56), channel_id=1, source_target_pairs={{16,0},{17,1},{18,2},{19,3},{20,4},{21,5},{22,6},{23,7},{24,8},{25... | collective-permute-start | bytes 215048 | tf_op jit(solution)/shard_map/ppermute | solution.py:527
  49.1 5.7 %copy-start = (f32[128,1024]{1,0:T(8,128)}, f32[128,1024]{1,0:T(8,128)S(1)}, u32[]{:S(2)}) copy-start(f32[128,1024]{1,0:T(8,128)S(1)} %get-tuple-element.64.dk_ref) | copy-start | bytes 1572868
  49.1 5.7 %copy-start.2 = (f32[128,1024]{1,0:T(8,128)}, f32[128,1024]{1,0:T(8,128)S(1)}, u32[]{:S(2)}) copy-start(f32[128,1024]{1,0:T(8,128)S(1)} %get-tuple-element.65.dv_ref) | copy-start | bytes 1572868
  51.4 23.1 %collective-permute-start.3 = (bf16[2,128,1024]{2,1,0:T(8,128)(2,1)}, bf16[2,128,1024]{2,1,0:T(8,128)(2,1)S(1)}, u32[]{:S(2)}, u32[]{:S(2)}) collective-permute-start(bf16[2,128,1024]{2,1,0:T(8,128)(2,1)} %get-tuple-element.66), channel_id=1, source_target_pairs={{1,0},{2,1},{3,2},{4,3},{5,4},{6,5},{7,6},{8,7},{9,8},{10,9},{11,1... | collective-permute-start | bytes 1572872 | tf_op jit(solution)/shard_map/ppermute | solution.py:531
  56.5 24.1 %all-to-all-start.1 = ((bf16[16,160,128]{2,1,0:T(8,128)(2,1)}), bf16[16,160,128]{2,1,0:T(8,128)(2,1)S(1)}, u32[]{:S(2)}, u32[]{:S(2)}) async-start(bf16[16,160,128]{2,1,0:T(8,128)(2,1)} %key_grads.1), calls=%async_computation.1 | async-start | bytes 1310720 | tf_op jit(solution)/shard_map/all_to_all | solution.py:533
  74.5 1.0 %copy-start.1 = (f32[128,1024]{1,0:T(8,128)S(1)}, f32[128,1024]{1,0:T(8,128)}, u32[]{:S(2)}) copy-start(f32[128,1024]{1,0:T(8,128)} %copy-done) | copy-start | bytes 1572868
  75.5 1.0 %copy-start.3 = (f32[128,1024]{1,0:T(8,128)S(1)}, f32[128,1024]{1,0:T(8,128)}, u32[]{:S(2)}) copy-start(f32[128,1024]{1,0:T(8,128)} %copy-done.2) | copy-start | bytes 1572868

commit v3 on v2

--- a/solution.py
+++ b/solution.py
@@ -160,7 +160,7 @@
         feat_ref[c] = feat
         ones = with_ones(rows_of(x_ref, c, 16, 80))
         run = run + nt(ones, feat)
-    total_ref[...] = run
+    total_ref[...] = run.astype(BF)
 
 
 def key_state(x):
@@ -169,7 +169,7 @@
         state_kernel,
         out_shape=(
             jax.ShapeDtypeStruct((STEPS, ROWS, FEAT), F32),
-            jax.ShapeDtypeStruct((ROWS, FEAT), F32),
+            jax.ShapeDtypeStruct((ROWS, FEAT), BF),
             feat,
         ),
         compiler_params=PARAMS,
@@ -221,7 +221,7 @@
     for c in range(STEPS):
         grads = rows_of(x_ref, c, 96, 160).astype(F32)
         feat = feat_ref[c]
-        state_hi, state_lo = split(pref_ref[c] + half_ref[...])
+        state_hi, state_lo = split(pref_ref[c] + half_ref[...].astype(F32))
         stack = nn(jnp.concatenate([state_hi, state_lo], 0), feat)
         numer = numer_ref[c] + stack[0:ROWS] + stack[ROWS:]
         inv = 1.0 / numer[64:65]
@@ -237,7 +237,7 @@
         lin_ref[c] = lin_out.astype(BF)
         dhi_ref[c] = d_hi
         dlo_ref[c] = d_lo
-    total_ref[...] = total
+    total_ref[...] = total.astype(BF)
 
 
 def output(x, pref, half, numer, feat):
@@ -249,7 +249,7 @@
             side,
             side,
             jax.ShapeDtypeStruct((STEPS, ROWS, FEAT), F32),
-            jax.ShapeDtypeStruct((ROWS, FEAT), F32),
+            jax.ShapeDtypeStruct((ROWS, FEAT), BF),
         ),
         compiler_params=PARAMS,
         name="linear_output",
@@ -268,7 +268,7 @@
         low_ref[c] = jnp.where(causal, d_kernel * (1.0 + scores_ref[c]), 0.0).astype(BF)
     for c in range(STEPS):
         d_hi, d_lo = dhi_ref[c], dlo_ref[c]
-        turned_hi, turned_lo = split(jnp.transpose(pref_ref[c] + half_ref[...]))
+        turned_hi, turned_lo = split(jnp.transpose(pref_ref[c] + half_ref[...].astype(F32)))
         feat_ref[c] = nn(turned_hi, d_hi) + nn(turned_lo, d_hi) + nn(turned_hi, d_lo)
     for c in range(STEPS):
         scores = scores_ref[c]
@@ -298,7 +298,7 @@
 
 
 def key_kernel(x_ref, lin_ref, dq_ref, part_ref, own_ref, half_ref, feat_ref, out_ref):
-    run = half_ref[...]
+    run = half_ref[...].astype(F32)
     for c in range(STEPS - 1, -1, -1):
         key = rows_of(x_ref, c, 0, 16).astype(F32)
         ones = with_ones(rows_of(x_ref, c, 16, 80))

time: 82.2 us -> 80.7 us (0.982)
  waiting for transfers between devices: 38 us -> 35.3 us
  starting transfers between devices: 25.6 us -> 26.5 us
    ppermute x1, waiting for transfers between devices: 13.1 us -> 11.7 us  [local(): back_halo = lax.ppermute(back_halo, seq, earlier)]
    all_to_all x1, starting transfers between devices: 4.81 us -> 5.7 us  [local(): y = spread(key_grads(x, lin, dq, part, state, next_half, key_feat))]
    ppermute x1, waiting for transfers between devices: 3.62 us -> 2.74 us  [local(): half = lax.ppermute(total, 'half', [(0, 1)])]
  transfers between devices with their start and end apart: 6 -> 6, of which waited for: 5 -> 5; matrix products, arithmetic and copies ran while one was open for 0% -> 0% of each run, Pallas kernels for 14% -> 15%
where the time goes in v3:
time: 80.7 us; the launch traced here: 80 us
  waiting for transfers between devices  35.3 us (44%)
  starting transfers between devices  26.5 us (33%)
  Pallas kernels  15.4 us (19%)
  local copies, waits for them, and re-layouts  2.09 us (3%)
    all_to_all x1, waiting for transfers between devices, local(): x = spread(own)  15.7 us
    ppermute x1, waiting for transfers between devices, local(): back_halo = lax.ppermute(back_halo, seq, earlier)  11.7 us
    all_to_all x1, starting transfers between devices, local(): x = spread(own)  9.59 us
    all_to_all x1, starting transfers between devices, local(): y = spread(key_grads(x, lin, dq, part, state, next_half, key_feat))  5.7 us
    ppermute x1, starting transfers between devices, local(): half = lax.ppermute(total, 'half', [(0, 1)])  4.8 us
    pallas_call x1, Pallas kernels, window(): pl.pallas_call(window_kernel, in_specs=[pl.BlockSpec(memory_space=pltpu.S...  4.35 us
    ppermute x1, starting transfers between devices, local(): halo = lax.ppermute(halo, seq, later)  3.85 us
    all_to_all x1, waiting for transfers between devices, local(): y = spread(key_grads(x, lin, dq, part, state, next_half, key_feat))  3.5 us
  transfers between devices with their start and end apart: 6, of which 5 were waited for; matrix products, arithmetic and copies ran while one was open for 0% of the time, Pallas kernels for 15%

profile of v3, /device:TPU:6, one launch (start us, length us, event | category | flops | bytes accessed | tf_op | source)
XLA Modules:
  0.0 80.0 jit_solution(6990345055614062947)
XLA Ops:
  0.6 2.7 %pack.1 = (bf16[16,160,128]{2,1,0:T(8,128)(2,1)}, bf16[2,128,1024]{2,1,0:T(8,128)(2,1)}) custom-call(bf16[128,256]{1,0:T(8,128)(2,1)} %ql_hbm.1, bf16[128,256]{1,0:T(8,128)(2,1)} %kl_hbm.1, bf16[128,1024]{1,0:T(8,128)(2,1)} %k_hbm.1, bf16[128,1024]{1,0:T(8,128)(2,1)} %v_hbm.3, bf16[128,1024]{1,0:T(8,128)(2,1)} %g_hbm.3), custom_call_target="tpu_custom_call" | custom-call | tf_op jit(solution)/shard_map/pack/pallas_call | solution.py:84
  3.3 9.6 %all-to-all-start = ((bf16[16,160,128]{2,1,0:T(8,128)(2,1)}), bf16[16,160,128]{2,1,0:T(8,128)(2,1)S(1)}, u32[]{:S(2)}, u32[]{:S(2)}) async-start(bf16[16,160,128]{2,1,0:T(8,128)(2,1)} %get-tuple-element.42), calls=%async_computation | async-start | bytes 1310720 | tf_op jit(solution)/shard_map/all_to_all | solution.py:520
  12.9 3.9 %collective-permute-start.1 = (bf16[2,128,1024]{2,1,0:T(8,128)(2,1)}, bf16[2,128,1024]{2,1,0:T(8,128)(2,1)S(1)}, u32[]{:S(2)}, u32[]{:S(2)}) collective-permute-start(bf16[2,128,1024]{2,1,0:T(8,128)(2,1)} %get-tuple-element.52), channel_id=1, source_target_pairs={{0,1},{1,2},{2,3},{3,4},{4,5},{5,6},{6,7},{7,8},{8,9},{9,10},{10,1... | collective-permute-start | bytes 1572872 | tf_op jit(solution)/shard_map/ppermute | solution.py:519
  16.8 15.7 %all-to-all-done.x_ref = bf16[16,160,128]{2,1,0:T(8,128)(2,1)S(1)} async-done(((bf16[16,160,128]{2,1,0:T(8,128)(2,1)}), bf16[16,160,128]{2,1,0:T(8,128)(2,1)S(1)}, u32[]{:S(2)}, u32[]{:S(2)}) %all-to-all-start) | async-done | bytes 655392 | tf_op jit(solution)/shard_map/all_to_all | solution.py:520
  32.5 0.4 key_state.1
  32.9 4.8 %collective-permute-start = (bf16[80,224]{1,0:T(8,128)(2,1)S(1)}, bf16[80,224]{1,0:T(8,128)(2,1)S(1)}, u32[]{:S(2)}, u32[]{:S(2)}) collective-permute-start(bf16[80,224]{1,0:T(8,128)(2,1)S(1)} %get-tuple-element.45), channel_id=1, source_target_pairs={{0,16},{1,17},{2,18},{3,19},{4,20},{5,21},{6,22},{7,23},{8,24},{9,... | collective-permute-start | bytes 107528 | tf_op jit(solution)/shard_map/ppermute | solution.py:523
  37.7 1.0 %inside_chunks.1 = (f32[8,256,256]{2,1,0:T(8,128)S(1)}, f32[8,80,256]{2,1,0:T(8,128)S(1)}, bf16[8,224,256]{2,1,0:T(8,128)(2,1)S(1)}) custom-call(bf16[16,160,128]{2,1,0:T(8,128)(2,1)S(1)} %all-to-all-done.x_ref), custom_call_target="tpu_custom_call" | custom-call | tf_op jit(solution)/shard_map/inside_chunks/pallas_call | solution.py:203
  38.8 2.7 %collective-permute-done.half_ref = bf16[80,224]{1,0:T(8,128)(2,1)S(1)} collective-permute-done((bf16[80,224]{1,0:T(8,128)(2,1)S(1)}, bf16[80,224]{1,0:T(8,128)(2,1)S(1)}, u32[]{:S(2)}, u32[]{:S(2)}) %collective-permute-start) | collective-permute-done | bytes 35872 | tf_op jit(solution)/shard_map/ppermute | solution.py:523
  41.5 1.1 %linear_output.1 = (bf16[8,64,256]{2,1,0:T(8,128)(2,1)S(1)}, bf16[8,80,256]{2,1,0:T(8,128)(2,1)S(1)}, bf16[8,80,256]{2,1,0:T(8,128)(2,1)S(1)}, f32[8,80,224]{2,1,0:T(8,128)S(1)}, bf16[80,224]{1,0:T(8,128)(2,1)S(1)}) custom-call(bf16[16,160,128]{2,1,0:T(8,128)(2,1)S(1)} %all-to-all-done.x_ref, f32[8,80,224]{2,1,0:T(8,128)S(1)} %get-tuple-element.43.pref_ref, ...), custom_call_target="tpu_custom_call" | custom-call | tf_op jit(solution)/shard_map/linear_output/pallas_call | solution.py:245
  42.6 0.0 collective-permute-done.1.halo_ref
  42.7 1.3 %collective-permute-start.2 = (bf16[80,224]{1,0:T(8,128)(2,1)S(1)}, bf16[80,224]{1,0:T(8,128)(2,1)S(1)}, u32[]{:S(2)}, u32[]{:S(2)}) collective-permute-start(bf16[80,224]{1,0:T(8,128)(2,1)S(1)} %get-tuple-element.56), channel_id=1, source_target_pairs={{16,0},{17,1},{18,2},{19,3},{20,4},{21,5},{22,6},{23,7},{24,8},{25... | collective-permute-start | bytes 107528 | tf_op jit(solution)/shard_map/ppermute | solution.py:527
  44.0 4.4 %window.1 = (f32[128,1024]{1,0:T(8,128)S(1)}, bf16[128,1024]{1,0:T(8,128)(2,1)}, f32[128,1024]{1,0:T(8,128)S(1)}, f32[128,1024]{1,0:T(8,128)S(1)}, bf16[2,128,1024]{2,1,0:T(8,128)(2,1)}) custom-call(s32[1]{0:T(128)} %bitcast.first_ref, bf16[128,1024]{1,0:T(8,128)(2,1)} %q_hbm.1, bf16[128,1024]{1,0:T(8,128)(2,1)} %k_hbm.1, bf16[128,1024]{1,0:T(8,128)(2,1)} %v_hbm.3, ...), custom_call_target="tpu_custom_call" | custom-call | flops 5000000000 | bytes 6000000 | tf_op jit(solution)/shard_map/window/pallas_call | solution.py:436
  48.3 0.0 copy-start
  48.3 0.0 copy-start.2
  48.3 1.7 %collective-permute-done.2.half_ref = bf16[80,224]{1,0:T(8,128)(2,1)S(1)} collective-permute-done((bf16[80,224]{1,0:T(8,128)(2,1)S(1)}, bf16[80,224]{1,0:T(8,128)(2,1)S(1)}, u32[]{:S(2)}, u32[]{:S(2)}) %collective-permute-start.2) | collective-permute-done | bytes 35872 | tf_op jit(solution)/shard_map/ppermute | solution.py:527
  50.1 1.3 %collective-permute-start.3 = (bf16[2,128,1024]{2,1,0:T(8,128)(2,1)}, bf16[2,128,1024]{2,1,0:T(8,128)(2,1)S(1)}, u32[]{:S(2)}, u32[]{:S(2)}) collective-permute-start(bf16[2,128,1024]{2,1,0:T(8,128)(2,1)} %get-tuple-element.66), channel_id=1, source_target_pairs={{1,0},{2,1},{3,2},{4,3},{5,4},{6,5},{7,6},{8,7},{9,8},{10,9},{11,1... | collective-permute-start | bytes 1572872 | tf_op jit(solution)/shard_map/ppermute | solution.py:531
  51.3 2.2 %query_grads.1 = (bf16[8,16,256]{2,1,0:T(8,128)(2,1)S(1)}, f32[8,80,256]{2,1,0:T(8,128)S(1)}) custom-call(bf16[16,160,128]{2,1,0:T(8,128)(2,1)S(1)} %all-to-all-done.x_ref, f32[8,256,256]{2,1,0:T(8,128)S(1)} %get-tuple-element.50.scores_ref, f32[8,80,224]{2,1,0:T(8,128)S(1)} %get-tuple-element.43.pref_ref, ...), custom_call_target="tpu_custom_call" | custom-call | tf_op jit(solution)/shard_map/query_grads/pallas_call | solution.py:285
  53.5 0.0 copy-done
  53.5 0.0 copy-done.2
  53.5 1.7 %key_grads.1 = bf16[16,160,128]{2,1,0:T(8,128)(2,1)} custom-call(bf16[16,160,128]{2,1,0:T(8,128)(2,1)S(1)} %all-to-all-done.x_ref, bf16[8,64,256]{2,1,0:T(8,128)(2,1)S(1)} %get-tuple-element.49.lin_ref, bf16[8,16,256]{2,1,0:T(8,128)(2,1)S(1)} %get-tuple-element.59.dq_ref, f32[8,80,256]{2,1,0:T(8,128)S(1)} %get-tuple-element.60.part_ref, ...), custom_call_target="tpu_custom_call" | custom-call | tf_op jit(solution)/shard_map/key_grads/pallas_call | solution.py:324
  55.3 5.7 %all-to-all-start.1 = ((bf16[16,160,128]{2,1,0:T(8,128)(2,1)}), bf16[16,160,128]{2,1,0:T(8,128)(2,1)S(1)}, u32[]{:S(2)}, u32[]{:S(2)}) async-start(bf16[16,160,128]{2,1,0:T(8,128)(2,1)} %key_grads.1), calls=%async_computation.1 | async-start | bytes 1310720 | tf_op jit(solution)/shard_map/all_to_all | solution.py:533
  61.0 11.7 %collective-permute-done.3.halo_ref = bf16[2,128,1024]{2,1,0:T(8,128)(2,1)S(1)} collective-permute-done((bf16[2,128,1024]{2,1,0:T(8,128)(2,1)}, bf16[2,128,1024]{2,1,0:T(8,128)(2,1)S(1)}, u32[]{:S(2)}, u32[]{:S(2)}) %collective-permute-start.3) | collective-permute-done | bytes 524320 | tf_op jit(solution)/shard_map/ppermute | solution.py:531
  72.6 0.0 copy-start.1
  72.6 1.0 %copy-done.1 = f32[128,1024]{1,0:T(8,128)S(1)} copy-done((f32[128,1024]{1,0:T(8,128)S(1)}, f32[128,1024]{1,0:T(8,128)}, u32[]{:S(2)}) %copy-start.1) | copy-done | bytes 524312
  73.7 0.0 copy-start.3
  73.7 1.0 %copy-done.3 = f32[128,1024]{1,0:T(8,128)S(1)} copy-done((f32[128,1024]{1,0:T(8,128)S(1)}, f32[128,1024]{1,0:T(8,128)}, u32[]{:S(2)}) %copy-start.3) | copy-done | bytes 524312
  74.7 0.8 %settle.1 = (bf16[128,1024]{1,0:T(8,128)(2,1)}, f32[128,1024]{1,0:T(8,128)S(1)}) custom-call(f32[128,1024]{1,0:T(8,128)S(1)} %copy-done.1, f32[128,1024]{1,0:T(8,128)S(1)} %copy-done.3, bf16[2,128,1024]{2,1,0:T(8,128)(2,1)S(1)} %collective-permute-done.3.halo_ref), custom_call_target="tpu_custom_call" | custom-call | flops 49999998976 | bytes 2000000 | tf_op jit(solution)/shard_map/settle/pallas_call | solution.py:473
  75.5 3.5 %all-to-all-done.1.y_ref = bf16[16,160,128]{2,1,0:T(8,128)(2,1)S(1)} async-done(((bf16[16,160,128]{2,1,0:T(8,128)(2,1)}), bf16[16,160,128]{2,1,0:T(8,128)(2,1)S(1)}, u32[]{:S(2)}, u32[]{:S(2)}) %all-to-all-start.1) | async-done | bytes 655392 | tf_op jit(solution)/shard_map/all_to_all | solution.py:533
  79.0 1.0 %finish.1 = (bf16[128,1024]{1,0:T(8,128)(2,1)}, bf16[128,256]{1,0:T(8,128)(2,1)}, bf16[128,256]{1,0:T(8,128)(2,1)}, bf16[128,1024]{1,0:T(8,128)(2,1)}) custom-call(bf16[16,160,128]{2,1,0:T(8,128)(2,1)S(1)} %all-to-all-done.1.y_ref, f32[128,1024]{1,0:T(8,128)S(1)} %get-tuple-element.70.out_ref, f32[128,1024]{1,0:T(8,128)S(1)} %get-tuple-element.71.dv_ref), custom_call_target="tpu_custom_call" | custom-call | tf_op jit(solution)/shard_map/finish/pallas_call | solution.py:503
Async XLA Ops:
  3.3 29.2 %all-to-all-start = ((bf16[16,160,128]{2,1,0:T(8,128)(2,1)}), bf16[16,160,128]{2,1,0:T(8,128)(2,1)S(1)}, u32[]{:S(2)}, u32[]{:S(2)}) async-start(bf16[16,160,128]{2,1,0:T(8,128)(2,1)} %get-tuple-element.42), calls=%async_computation | async-start | bytes 1310720 | tf_op jit(solution)/shard_map/all_to_all | solution.py:520
  12.9 29.7 %collective-permute-start.1 = (bf16[2,128,1024]{2,1,0:T(8,128)(2,1)}, bf16[2,128,1024]{2,1,0:T(8,128)(2,1)S(1)}, u32[]{:S(2)}, u32[]{:S(2)}) collective-permute-start(bf16[2,128,1024]{2,1,0:T(8,128)(2,1)} %get-tuple-element.52), channel_id=1, source_target_pairs={{0,1},{1,2},{2,3},{3,4},{4,5},{5,6},{6,7},{7,8},{8,9},{9,10},{10,1... | collective-permute-start | bytes 1572872 | tf_op jit(solution)/shard_map/ppermute | solution.py:519
  32.9 8.6 %collective-permute-start = (bf16[80,224]{1,0:T(8,128)(2,1)S(1)}, bf16[80,224]{1,0:T(8,128)(2,1)S(1)}, u32[]{:S(2)}, u32[]{:S(2)}) collective-permute-start(bf16[80,224]{1,0:T(8,128)(2,1)S(1)} %get-tuple-element.45), channel_id=1, source_target_pairs={{0,16},{1,17},{2,18},{3,19},{4,20},{5,21},{6,22},{7,23},{8,24},{9,... | collective-permute-start | bytes 107528 | tf_op jit(solution)/shard_map/ppermute | solution.py:523
  42.7 7.4 %collective-permute-start.2 = (bf16[80,224]{1,0:T(8,128)(2,1)S(1)}, bf16[80,224]{1,0:T(8,128)(2,1)S(1)}, u32[]{:S(2)}, u32[]{:S(2)}) collective-permute-start(bf16[80,224]{1,0:T(8,128)(2,1)S(1)} %get-tuple-element.56), channel_id=1, source_target_pairs={{16,0},{17,1},{18,2},{19,3},{20,4},{21,5},{22,6},{23,7},{24,8},{25... | collective-permute-start | bytes 107528 | tf_op jit(solution)/shard_map/ppermute | solution.py:527
  48.3 5.2 %copy-start = (f32[128,1024]{1,0:T(8,128)}, f32[128,1024]{1,0:T(8,128)S(1)}, u32[]{:S(2)}) copy-start(f32[128,1024]{1,0:T(8,128)S(1)} %get-tuple-element.64.dk_ref) | copy-start | bytes 1572868
  48.3 5.2 %copy-start.2 = (f32[128,1024]{1,0:T(8,128)}, f32[128,1024]{1,0:T(8,128)S(1)}, u32[]{:S(2)}) copy-start(f32[128,1024]{1,0:T(8,128)S(1)} %get-tuple-element.65.dv_ref) | copy-start | bytes 1572868
  50.1 22.6 %collective-permute-start.3 = (bf16[2,128,1024]{2,1,0:T(8,128)(2,1)}, bf16[2,128,1024]{2,1,0:T(8,128)(2,1)S(1)}, u32[]{:S(2)}, u32[]{:S(2)}) collective-permute-start(bf16[2,128,1024]{2,1,0:T(8,128)(2,1)} %get-tuple-element.66), channel_id=1, source_target_pairs={{1,0},{2,1},{3,2},{4,3},{5,4},{6,5},{7,6},{8,7},{9,8},{10,9},{11,1... | collective-permute-start | bytes 1572872 | tf_op jit(solution)/shard_map/ppermute | solution.py:531
  55.3 23.7 %all-to-all-start.1 = ((bf16[16,160,128]{2,1,0:T(8,128)(2,1)}), bf16[16,160,128]{2,1,0:T(8,128)(2,1)S(1)}, u32[]{:S(2)}, u32[]{:S(2)}) async-start(bf16[16,160,128]{2,1,0:T(8,128)(2,1)} %key_grads.1), calls=%async_computation.1 | async-start | bytes 1310720 | tf_op jit(solution)/shard_map/all_to_all | solution.py:533
  72.6 1.0 %copy-start.1 = (f32[128,1024]{1,0:T(8,128)S(1)}, f32[128,1024]{1,0:T(8,128)}, u32[]{:S(2)}) copy-start(f32[128,1024]{1,0:T(8,128)} %copy-done) | copy-start | bytes 1572868
  73.7 1.0 %copy-start.3 = (f32[128,1024]{1,0:T(8,128)S(1)}, f32[128,1024]{1,0:T(8,128)}, u32[]{:S(2)}) copy-start(f32[128,1024]{1,0:T(8,128)} %copy-done.2) | copy-start | bytes 1572868

commit v4 on v3

--- a/solution.py
+++ b/solution.py
@@ -297,7 +297,8 @@
     )(x, scores, pref, half, d_hi, d_lo)
 
 
-def key_kernel(x_ref, lin_ref, dq_ref, part_ref, own_ref, half_ref, feat_ref, out_ref):
+def key_kernel(x_ref, lin_ref, dq_ref, part_ref, own_ref, half_ref, feat_ref, out_hbm, out_ref, sems):
+    copies = []
     run = half_ref[...].astype(F32)
     for c in range(STEPS - 1, -1, -1):
         key = rows_of(x_ref, c, 0, 16).astype(F32)
@@ -316,14 +317,24 @@
             out_ref[2 * c + i, 64:80] = dq_ref[c, :, cols]
             out_ref[2 * c + i, 80:144] = d_value[:, cols]
             out_ref[2 * c + i, 144:160] = d_key[:, cols]
+        rows = pl.ds(2 * c, 2)
+        copies.append(pltpu.make_async_copy(out_ref.at[rows], out_hbm.at[rows], sems.at[c]))
+        copies[-1].start()
         if c:
             run = run + own_ref[c]
+    for copy in copies:
+        copy.wait()
 
 
 def key_grads(x, lin, dq, part, own, half, feat):
     return pl.pallas_call(
         key_kernel,
+        out_specs=pl.BlockSpec(memory_space=pltpu.HBM),
         out_shape=jax.ShapeDtypeStruct((H, 2 * ROWS, TOK), BF),
+        scratch_shapes=[
+            pltpu.VMEM((H, 2 * ROWS, TOK), BF),
+            pltpu.SemaphoreType.DMA((STEPS,)),
+        ],
         compiler_params=PARAMS,
         name="key_grads",
     )(x, lin, dq, part, own, half, feat)
@@ -383,17 +394,17 @@
     for p in pairs:
         scores = nt(key_rows(p), query_rows(p))
         logit_ref[p] = jnp.where(own, scores[0:TOK], scores[TOK:] + blocked)
-    copies[2].wait()
-    copies[3].wait()
-    for p in pairs:
-        d_both = nt(value_rows(p), grad_rows(p))
-        d_attn_ref[p] = jnp.where(own, d_both[0:TOK], d_both[TOK:])
     for p in pairs:
         logits = logit_ref[p]
         shifted = jnp.exp(logits - jnp.max(logits, 0, keepdims=True))
         attn = shifted * (1.0 / jnp.sum(shifted, 0, keepdims=True))
         logit_ref[p] = attn
         low_ref[p] = attn.astype(BF)
+    copies[2].wait()
+    copies[3].wait()
+    for p in pairs:
+        d_both = nt(value_rows(p), grad_rows(p))
+        d_attn_ref[p] = jnp.where(own, d_both[0:TOK], d_both[TOK:])
     for p in pairs:
         pieces = []
         for i in range(2):

time: 80.7 us -> 80.7 us (level)
  transfers between devices with their start and end apart: 6 -> 6, of which waited for: 5 -> 5; matrix products, arithmetic and copies ran while one was open for 0% -> 0% of each run, Pallas kernels for 15% -> 14%
where the time goes in v4:
time: 80.7 us; the launch traced here: 80 us
  waiting for transfers between devices  35.4 us (44%)
  starting transfers between devices  26.5 us (33%)
  Pallas kernels  15.3 us (19%)
  local copies, waits for them, and re-layouts  2.09 us (3%)
    all_to_all x1, waiting for transfers between devices, local(): x = spread(own)  15.7 us
    ppermute x1, waiting for transfers between devices, local(): back_halo = lax.ppermute(back_halo, seq, earlier)  11.7 us
    all_to_all x1, starting transfers between devices, local(): x = spread(own)  9.59 us
    all_to_all x1, starting transfers between devices, local(): y = spread(key_grads(x, lin, dq, part, state, next_half, key_feat))  5.72 us
    ppermute x1, starting transfers between devices, local(): half = lax.ppermute(total, 'half', [(0, 1)])  4.8 us
    pallas_call x1, Pallas kernels, window(): pl.pallas_call(window_kernel, in_specs=[pl.BlockSpec(memory_space=pltpu.S...  4.37 us
    ppermute x1, starting transfers between devices, local(): halo = lax.ppermute(halo, seq, later)  3.85 us
    all_to_all x1, waiting for transfers between devices, local(): y = spread(key_grads(x, lin, dq, part, state, next_half, key_feat))  3.5 us
  transfers between devices with their start and end apart: 6, of which 5 were waited for; matrix products, arithmetic and copies ran while one was open for 0% of the time, Pallas kernels for 14%

profile of v4, /device:TPU:6, one launch (start us, length us, event | category | flops | bytes accessed | tf_op | source)
XLA Modules:
  0.0 80.0 jit_solution(17068090131169727327)
XLA Ops:
  0.6 2.7 %pack.1 = (bf16[16,160,128]{2,1,0:T(8,128)(2,1)}, bf16[2,128,1024]{2,1,0:T(8,128)(2,1)}) custom-call(bf16[128,256]{1,0:T(8,128)(2,1)} %ql_hbm.1, bf16[128,256]{1,0:T(8,128)(2,1)} %kl_hbm.1, bf16[128,1024]{1,0:T(8,128)(2,1)} %k_hbm.1, bf16[128,1024]{1,0:T(8,128)(2,1)} %v_hbm.3, bf16[128,1024]{1,0:T(8,128)(2,1)} %g_hbm.3), custom_call_target="tpu_custom_call" | custom-call | tf_op jit(solution)/shard_map/pack/pallas_call | solution.py:84
  3.3 9.6 %all-to-all-start = ((bf16[16,160,128]{2,1,0:T(8,128)(2,1)}), bf16[16,160,128]{2,1,0:T(8,128)(2,1)S(1)}, u32[]{:S(2)}, u32[]{:S(2)}) async-start(bf16[16,160,128]{2,1,0:T(8,128)(2,1)} %get-tuple-element.42), calls=%async_computation | async-start | bytes 1310720 | tf_op jit(solution)/shard_map/all_to_all | solution.py:531
  12.9 3.9 %collective-permute-start.1 = (bf16[2,128,1024]{2,1,0:T(8,128)(2,1)}, bf16[2,128,1024]{2,1,0:T(8,128)(2,1)S(1)}, u32[]{:S(2)}, u32[]{:S(2)}) collective-permute-start(bf16[2,128,1024]{2,1,0:T(8,128)(2,1)} %get-tuple-element.52), channel_id=1, source_target_pairs={{0,1},{1,2},{2,3},{3,4},{4,5},{5,6},{6,7},{7,8},{8,9},{9,10},{10,1... | collective-permute-start | bytes 1572872 | tf_op jit(solution)/shard_map/ppermute | solution.py:530
  16.8 15.7 %all-to-all-done.x_ref = bf16[16,160,128]{2,1,0:T(8,128)(2,1)S(1)} async-done(((bf16[16,160,128]{2,1,0:T(8,128)(2,1)}), bf16[16,160,128]{2,1,0:T(8,128)(2,1)S(1)}, u32[]{:S(2)}, u32[]{:S(2)}) %all-to-all-start) | async-done | bytes 655392 | tf_op jit(solution)/shard_map/all_to_all | solution.py:531
  32.5 0.4 key_state.1
  32.9 4.8 %collective-permute-start = (bf16[80,224]{1,0:T(8,128)(2,1)S(1)}, bf16[80,224]{1,0:T(8,128)(2,1)S(1)}, u32[]{:S(2)}, u32[]{:S(2)}) collective-permute-start(bf16[80,224]{1,0:T(8,128)(2,1)S(1)} %get-tuple-element.45), channel_id=1, source_target_pairs={{0,16},{1,17},{2,18},{3,19},{4,20},{5,21},{6,22},{7,23},{8,24},{9,... | collective-permute-start | bytes 107528 | tf_op jit(solution)/shard_map/ppermute | solution.py:534
  37.7 1.0 %inside_chunks.1 = (f32[8,256,256]{2,1,0:T(8,128)S(1)}, f32[8,80,256]{2,1,0:T(8,128)S(1)}, bf16[8,224,256]{2,1,0:T(8,128)(2,1)S(1)}) custom-call(bf16[16,160,128]{2,1,0:T(8,128)(2,1)S(1)} %all-to-all-done.x_ref), custom_call_target="tpu_custom_call" | custom-call | tf_op jit(solution)/shard_map/inside_chunks/pallas_call | solution.py:203
  38.8 2.7 %collective-permute-done.half_ref = bf16[80,224]{1,0:T(8,128)(2,1)S(1)} collective-permute-done((bf16[80,224]{1,0:T(8,128)(2,1)S(1)}, bf16[80,224]{1,0:T(8,128)(2,1)S(1)}, u32[]{:S(2)}, u32[]{:S(2)}) %collective-permute-start) | collective-permute-done | bytes 35872 | tf_op jit(solution)/shard_map/ppermute | solution.py:534
  41.5 1.1 %linear_output.1 = (bf16[8,64,256]{2,1,0:T(8,128)(2,1)S(1)}, bf16[8,80,256]{2,1,0:T(8,128)(2,1)S(1)}, bf16[8,80,256]{2,1,0:T(8,128)(2,1)S(1)}, f32[8,80,224]{2,1,0:T(8,128)S(1)}, bf16[80,224]{1,0:T(8,128)(2,1)S(1)}) custom-call(bf16[16,160,128]{2,1,0:T(8,128)(2,1)S(1)} %all-to-all-done.x_ref, f32[8,80,224]{2,1,0:T(8,128)S(1)} %get-tuple-element.43.pref_ref, ...), custom_call_target="tpu_custom_call" | custom-call | tf_op jit(solution)/shard_map/linear_output/pallas_call | solution.py:245
  42.6 0.0 collective-permute-done.1.halo_ref
  42.7 1.3 %collective-permute-start.2 = (bf16[80,224]{1,0:T(8,128)(2,1)S(1)}, bf16[80,224]{1,0:T(8,128)(2,1)S(1)}, u32[]{:S(2)}, u32[]{:S(2)}) collective-permute-start(bf16[80,224]{1,0:T(8,128)(2,1)S(1)} %get-tuple-element.56), channel_id=1, source_target_pairs={{16,0},{17,1},{18,2},{19,3},{20,4},{21,5},{22,6},{23,7},{24,8},{25... | collective-permute-start | bytes 107528 | tf_op jit(solution)/shard_map/ppermute | solution.py:538
  44.0 4.4 %window.1 = (f32[128,1024]{1,0:T(8,128)S(1)}, bf16[128,1024]{1,0:T(8,128)(2,1)}, f32[128,1024]{1,0:T(8,128)S(1)}, f32[128,1024]{1,0:T(8,128)S(1)}, bf16[2,128,1024]{2,1,0:T(8,128)(2,1)}) custom-call(s32[1]{0:T(128)} %bitcast.first_ref, bf16[128,1024]{1,0:T(8,128)(2,1)} %q_hbm.1, bf16[128,1024]{1,0:T(8,128)(2,1)} %k_hbm.1, bf16[128,1024]{1,0:T(8,128)(2,1)} %v_hbm.3, ...), custom_call_target="tpu_custom_call" | custom-call | flops 5000000000 | bytes 6000000 | tf_op jit(solution)/shard_map/window/pallas_call | solution.py:447
  48.3 0.0 copy-start
  48.3 0.0 copy-start.2
  48.4 1.7 %collective-permute-done.2.half_ref = bf16[80,224]{1,0:T(8,128)(2,1)S(1)} collective-permute-done((bf16[80,224]{1,0:T(8,128)(2,1)S(1)}, bf16[80,224]{1,0:T(8,128)(2,1)S(1)}, u32[]{:S(2)}, u32[]{:S(2)}) %collective-permute-start.2) | collective-permute-done | bytes 35872 | tf_op jit(solution)/shard_map/ppermute | solution.py:538
  50.1 1.3 %collective-permute-start.3 = (bf16[2,128,1024]{2,1,0:T(8,128)(2,1)}, bf16[2,128,1024]{2,1,0:T(8,128)(2,1)S(1)}, u32[]{:S(2)}, u32[]{:S(2)}) collective-permute-start(bf16[2,128,1024]{2,1,0:T(8,128)(2,1)} %get-tuple-element.66), channel_id=1, source_target_pairs={{1,0},{2,1},{3,2},{4,3},{5,4},{6,5},{7,6},{8,7},{9,8},{10,9},{11,1... | collective-permute-start | bytes 1572872 | tf_op jit(solution)/shard_map/ppermute | solution.py:542
  51.3 2.2 %query_grads.1 = (bf16[8,16,256]{2,1,0:T(8,128)(2,1)S(1)}, f32[8,80,256]{2,1,0:T(8,128)S(1)}) custom-call(bf16[16,160,128]{2,1,0:T(8,128)(2,1)S(1)} %all-to-all-done.x_ref, f32[8,256,256]{2,1,0:T(8,128)S(1)} %get-tuple-element.50.scores_ref, f32[8,80,224]{2,1,0:T(8,128)S(1)} %get-tuple-element.43.pref_ref, ...), custom_call_target="tpu_custom_call" | custom-call | tf_op jit(solution)/shard_map/query_grads/pallas_call | solution.py:285
  53.5 0.0 copy-done
  53.5 0.0 copy-done.2
  53.5 1.6 %key_grads.1 = bf16[16,160,128]{2,1,0:T(8,128)(2,1)} custom-call(bf16[16,160,128]{2,1,0:T(8,128)(2,1)S(1)} %all-to-all-done.x_ref, bf16[8,64,256]{2,1,0:T(8,128)(2,1)S(1)} %get-tuple-element.49.lin_ref, bf16[8,16,256]{2,1,0:T(8,128)(2,1)S(1)} %get-tuple-element.59.dq_ref, f32[8,80,256]{2,1,0:T(8,128)S(1)} %get-tuple-element.60.part_ref, ...), custom_call_target="tpu_custom_call" | custom-call | tf_op jit(solution)/shard_map/key_grads/pallas_call | solution.py:330
  55.2 5.7 %all-to-all-start.1 = ((bf16[16,160,128]{2,1,0:T(8,128)(2,1)}), bf16[16,160,128]{2,1,0:T(8,128)(2,1)S(1)}, u32[]{:S(2)}, u32[]{:S(2)}) async-start(bf16[16,160,128]{2,1,0:T(8,128)(2,1)} %key_grads.1), calls=%async_computation.1 | async-start | bytes 1310720 | tf_op jit(solution)/shard_map/all_to_all | solution.py:544
  60.9 11.7 %collective-permute-done.3.halo_ref = bf16[2,128,1024]{2,1,0:T(8,128)(2,1)S(1)} collective-permute-done((bf16[2,128,1024]{2,1,0:T(8,128)(2,1)}, bf16[2,128,1024]{2,1,0:T(8,128)(2,1)S(1)}, u32[]{:S(2)}, u32[]{:S(2)}) %collective-permute-start.3) | collective-permute-done | bytes 524320 | tf_op jit(solution)/shard_map/ppermute | solution.py:542
  72.6 0.0 copy-start.1
  72.6 1.0 %copy-done.1 = f32[128,1024]{1,0:T(8,128)S(1)} copy-done((f32[128,1024]{1,0:T(8,128)S(1)}, f32[128,1024]{1,0:T(8,128)}, u32[]{:S(2)}) %copy-start.1) | copy-done | bytes 524312
  73.7 0.0 copy-start.3
  73.7 1.0 %copy-done.3 = f32[128,1024]{1,0:T(8,128)S(1)} copy-done((f32[128,1024]{1,0:T(8,128)S(1)}, f32[128,1024]{1,0:T(8,128)}, u32[]{:S(2)}) %copy-start.3) | copy-done | bytes 524312
  74.7 0.8 %settle.1 = (bf16[128,1024]{1,0:T(8,128)(2,1)}, f32[128,1024]{1,0:T(8,128)S(1)}) custom-call(f32[128,1024]{1,0:T(8,128)S(1)} %copy-done.1, f32[128,1024]{1,0:T(8,128)S(1)} %copy-done.3, bf16[2,128,1024]{2,1,0:T(8,128)(2,1)S(1)} %collective-permute-done.3.halo_ref), custom_call_target="tpu_custom_call" | custom-call | flops 49999998976 | bytes 2000000 | tf_op jit(solution)/shard_map/settle/pallas_call | solution.py:484
  75.5 3.5 %all-to-all-done.1.y_ref = bf16[16,160,128]{2,1,0:T(8,128)(2,1)S(1)} async-done(((bf16[16,160,128]{2,1,0:T(8,128)(2,1)}), bf16[16,160,128]{2,1,0:T(8,128)(2,1)S(1)}, u32[]{:S(2)}, u32[]{:S(2)}) %all-to-all-start.1) | async-done | bytes 655392 | tf_op jit(solution)/shard_map/all_to_all | solution.py:544
  79.0 1.0 %finish.1 = (bf16[128,1024]{1,0:T(8,128)(2,1)}, bf16[128,256]{1,0:T(8,128)(2,1)}, bf16[128,256]{1,0:T(8,128)(2,1)}, bf16[128,1024]{1,0:T(8,128)(2,1)}) custom-call(bf16[16,160,128]{2,1,0:T(8,128)(2,1)S(1)} %all-to-all-done.1.y_ref, f32[128,1024]{1,0:T(8,128)S(1)} %get-tuple-element.70.out_ref, f32[128,1024]{1,0:T(8,128)S(1)} %get-tuple-element.71.dv_ref), custom_call_target="tpu_custom_call" | custom-call | tf_op jit(solution)/shard_map/finish/pallas_call | solution.py:514
Async XLA Ops:
  3.3 29.2 %all-to-all-start = ((bf16[16,160,128]{2,1,0:T(8,128)(2,1)}), bf16[16,160,128]{2,1,0:T(8,128)(2,1)S(1)}, u32[]{:S(2)}, u32[]{:S(2)}) async-start(bf16[16,160,128]{2,1,0:T(8,128)(2,1)} %get-tuple-element.42), calls=%async_computation | async-start | bytes 1310720 | tf_op jit(solution)/shard_map/all_to_all | solution.py:531
  12.9 29.7 %collective-permute-start.1 = (bf16[2,128,1024]{2,1,0:T(8,128)(2,1)}, bf16[2,128,1024]{2,1,0:T(8,128)(2,1)S(1)}, u32[]{:S(2)}, u32[]{:S(2)}) collective-permute-start(bf16[2,128,1024]{2,1,0:T(8,128)(2,1)} %get-tuple-element.52), channel_id=1, source_target_pairs={{0,1},{1,2},{2,3},{3,4},{4,5},{5,6},{6,7},{7,8},{8,9},{9,10},{10,1... | collective-permute-start | bytes 1572872 | tf_op jit(solution)/shard_map/ppermute | solution.py:530
  32.9 8.6 %collective-permute-start = (bf16[80,224]{1,0:T(8,128)(2,1)S(1)}, bf16[80,224]{1,0:T(8,128)(2,1)S(1)}, u32[]{:S(2)}, u32[]{:S(2)}) collective-permute-start(bf16[80,224]{1,0:T(8,128)(2,1)S(1)} %get-tuple-element.45), channel_id=1, source_target_pairs={{0,16},{1,17},{2,18},{3,19},{4,20},{5,21},{6,22},{7,23},{8,24},{9,... | collective-permute-start | bytes 107528 | tf_op jit(solution)/shard_map/ppermute | solution.py:534
  42.7 7.4 %collective-permute-start.2 = (bf16[80,224]{1,0:T(8,128)(2,1)S(1)}, bf16[80,224]{1,0:T(8,128)(2,1)S(1)}, u32[]{:S(2)}, u32[]{:S(2)}) collective-permute-start(bf16[80,224]{1,0:T(8,128)(2,1)S(1)} %get-tuple-element.56), channel_id=1, source_target_pairs={{16,0},{17,1},{18,2},{19,3},{20,4},{21,5},{22,6},{23,7},{24,8},{25... | collective-permute-start | bytes 107528 | tf_op jit(solution)/shard_map/ppermute | solution.py:538
  48.3 5.2 %copy-start = (f32[128,1024]{1,0:T(8,128)}, f32[128,1024]{1,0:T(8,128)S(1)}, u32[]{:S(2)}) copy-start(f32[128,1024]{1,0:T(8,128)S(1)} %get-tuple-element.64.dk_ref) | copy-start | bytes 1572868
  48.3 5.2 %copy-start.2 = (f32[128,1024]{1,0:T(8,128)}, f32[128,1024]{1,0:T(8,128)S(1)}, u32[]{:S(2)}) copy-start(f32[128,1024]{1,0:T(8,128)S(1)} %get-tuple-element.65.dv_ref) | copy-start | bytes 1572868
  50.1 22.6 %collective-permute-start.3 = (bf16[2,128,1024]{2,1,0:T(8,128)(2,1)}, bf16[2,128,1024]{2,1,0:T(8,128)(2,1)S(1)}, u32[]{:S(2)}, u32[]{:S(2)}) collective-permute-start(bf16[2,128,1024]{2,1,0:T(8,128)(2,1)} %get-tuple-element.66), channel_id=1, source_target_pairs={{1,0},{2,1},{3,2},{4,3},{5,4},{6,5},{7,6},{8,7},{9,8},{10,9},{11,1... | collective-permute-start | bytes 1572872 | tf_op jit(solution)/shard_map/ppermute | solution.py:542
  55.2 23.8 %all-to-all-start.1 = ((bf16[16,160,128]{2,1,0:T(8,128)(2,1)}), bf16[16,160,128]{2,1,0:T(8,128)(2,1)S(1)}, u32[]{:S(2)}, u32[]{:S(2)}) async-start(bf16[16,160,128]{2,1,0:T(8,128)(2,1)} %key_grads.1), calls=%async_computation.1 | async-start | bytes 1310720 | tf_op jit(solution)/shard_map/all_to_all | solution.py:544
  72.6 1.0 %copy-start.1 = (f32[128,1024]{1,0:T(8,128)S(1)}, f32[128,1024]{1,0:T(8,128)}, u32[]{:S(2)}) copy-start(f32[128,1024]{1,0:T(8,128)} %copy-done) | copy-start | bytes 1572868
  73.7 1.0 %copy-start.3 = (f32[128,1024]{1,0:T(8,128)S(1)}, f32[128,1024]{1,0:T(8,128)}, u32[]{:S(2)}) copy-start(f32[128,1024]{1,0:T(8,128)} %copy-done.2) | copy-start | bytes 1572868
